TPU v7x, 256 devices: a whole 4x4x8 slice. The times are simulated.
256 devices in a mesh: wide: 16 (over y, z_hi), narrow: 16 (over x, z_lo, core).
Axes of the slice: x: 4, y: 4, z: 8 (z_hi: 4, z_lo: 2; z = z_hi * 2 + z_lo), core: 2. Of those that a mesh axis runs over, the one named last changes fastest.
Arguments:
- features: bfloat16 [65536, 768], P(('wide', 'narrow'))
- proj_weight: bfloat16 [768, 512], replicated, may hold values from -0.21875 to 0.21875
- bias: float32 [512], replicated, may hold values from -1.5 to 1.5
- disc_weight: float32 [512, 512], replicated, may hold values from -0.25 to 0.25
- adjacency: int32 [16, 16, 24, 256, 256], P('wide', 'narrow'), may hold values from 0 to 3
- row_block: int32 [16, 16, 24], P('wide', 'narrow'), may hold values from 0 to 15
- col_block: int32 [16, 16, 24], P('wide', 'narrow'), may hold values from 0 to 15
- block_count: int32 [16, 16], P('wide', 'narrow'), may hold values from 1 to 24, as said below
- degree: int32 [65536], replicated, may hold values from 6 to 65
- corrupt_source: int32 [256], replicated, may hold values from 0 to 255, as said below
Outputs:
- hidden: bfloat16 [65536, 512], P(('wide', 'narrow'))
- scores: float32 [2, 65536], P(None, ('wide', 'narrow'))
- loss: float32 [], replicated
Inputs may be any that keep to these rules, and one draw needn't show every extreme that they name: Only slots below block_count of a tile take part; some tile holds 24 live slots in every draw. corrupt_source is a permutation of the blocks, and block g and block corrupt_source[g] have equal g % 16.
All inputs are finite; a program needn't handle non-finite values.
Results may differ from a plain program's by a relative error of at most 0.0056.
Values may be sent and summed in bfloat16 or wider, within the bound.
No kernel may reach another device: no remote copies, remote signals or barrier semaphores. Data moves between devices by JAX's collectives and lax.ppermute only.
A program may use at most 128 MiB of HBM per device.

v0:
```python
import functools

import jax
import jax.numpy as jnp
from jax import lax
from jax.experimental import pallas as pl
from jax.experimental.pallas import tpu as pltpu
from jax.sharding import PartitionSpec as P


X, ZL, CORES = 4, 2, 2
Y, ZH = 4, 4
BOTH = ("wide", "narrow")


def narrow_perm(dx=0, flip_z=0, flip_core=0):
    pairs = []
    for x in range(X):
        for zl in range(ZL):
            for core in range(CORES):
                target = (((x + dx) % X) * ZL + (zl ^ flip_z)) * CORES + (core ^ flip_core)
                pairs.append(((x * ZL + zl) * CORES + core, target))
    return pairs


def wide_perm(dy=0, dz=0):
    return [
        (y * ZH + zh, ((y + dy) % Y) * ZH + (zh + dz) % ZH) for y in range(Y) for zh in range(ZH)
    ]


def to_narrow(value, **steps):
    return lax.ppermute(value, "narrow", narrow_perm(**steps))


def to_wide(value, **steps):
    return lax.ppermute(value, "wide", wide_perm(**steps))


SLOTS = 24
ORDER, COL, SRC, START, ROWS, DEST, OWN = 0, 24, 48, 72, 89, 105, 121
META = 128
GRANT = 60 * 1024 * 1024


def spmm_kernel(meta, normed, *refs):
    pieces, (sent, kept, own), (panel, blocks, acc, sem) = refs[:Y], refs[Y : Y + 3], refs[Y + 3 :]
    step = pl.program_id(0)
    rows = pl.num_programs(0) // 2
    width = panel.shape[2]

    @pl.when(step == 0)
    def _():
        copies = [pltpu.make_async_copy(normed, blocks, sem.at[Y * ZH])]
        for k in range(Y):
            for j in range(ZH):
                target = panel.at[meta[DEST + k * ZH + j]]
                copies.append(pltpu.make_async_copy(pieces[k].at[j], target, sem.at[k * ZH + j]))
        for copy in copies:
            copy.start()
        for copy in copies:
            copy.wait()
        own[...] = panel[meta[OWN]]

    row = meta[ROWS + step]
    first = meta[START + row]
    count = meta[START + row + 1] - first

    def product(at):
        slot = meta[ORDER + at]
        block = blocks[slot]
        clean = jnp.dot(block, panel[meta[COL + slot]], preferred_element_type=jnp.float32)
        corrupt = jnp.dot(block, panel[meta[SRC + slot]], preferred_element_type=jnp.float32)
        return clean, corrupt

    def write(out):
        @pl.when(count == 0)
        def _():
            out[...] = jnp.zeros_like(out)

        @pl.when(count == 1)
        def _():
            clean, corrupt = product(first)
            out[0, :, :width] = clean.astype(out.dtype)
            out[0, :, width:] = corrupt.astype(out.dtype)

        @pl.when(count > 1)
        def _():
            acc[:, :width], acc[:, width:] = product(first)

            def add_slot(at, carry):
                clean, corrupt = product(at)
                acc[:, :width] += clean
                acc[:, width:] += corrupt
                return carry

            lax.fori_loop(first + 1, first + count, add_slot, 0)
            out[0] = acc[...].astype(out.dtype)

    @pl.when(step < rows)
    def _():
        write(sent)

    @pl.when(step >= rows)
    def _():
        write(kept)


def spmm(meta, normed, pieces):
    slots, block_len, _ = normed.shape
    width = pieces[0].shape[2]
    rows = X * ZL
    half = jax.ShapeDtypeStruct((rows, block_len, 2 * width), jnp.bfloat16)
    return pl.pallas_call(
        spmm_kernel,
        grid=(2 * rows,),
        in_specs=[pl.BlockSpec(memory_space=pltpu.SMEM)]
        + [pl.BlockSpec(memory_space=pl.ANY)] * (1 + len(pieces)),
        out_specs=[
            pl.BlockSpec((1, block_len, 2 * width), lambda i: (jnp.minimum(i, rows - 1), 0, 0)),
            pl.BlockSpec((1, block_len, 2 * width), lambda i: (jnp.maximum(i - rows, 0), 0, 0)),
            pl.BlockSpec((block_len, width), lambda i: (0, 0)),
        ],
        out_shape=[half, half, jax.ShapeDtypeStruct((block_len, width), jnp.bfloat16)],
        scratch_shapes=[
            pltpu.VMEM((Y * ZH, block_len, width), jnp.bfloat16),
            pltpu.VMEM(normed.shape, normed.dtype),
            pltpu.VMEM((block_len, 2 * width), jnp.float32),
            pltpu.SemaphoreType.DMA((Y * ZH + 1,)),
        ],
        compiler_params=pltpu.CompilerParams(vmem_limit_bytes=GRANT),
        cost_estimate=pl.CostEstimate(
            flops=slots * block_len * block_len * 4 * width,
            bytes_accessed=10 * 1024 * 1024,
            transcendentals=0,
        ),
    )(meta, normed, *pieces)


def pair_kernel(kept, arrived, *outs):
    total = kept[...].astype(jnp.float32) + arrived[...].astype(jnp.float32)
    for k, out in enumerate(outs):
        out[...] = total[k].astype(out.dtype)


def pair_sum(kept, arrived):
    rows, block_len, width = kept.shape
    part = block_len // 2
    shape = (X, ZL, block_len, width)
    return pl.pallas_call(
        pair_kernel,
        grid=(ZL, 2),
        in_specs=[pl.BlockSpec((X, 1, part, width), lambda i, j: (0, i, j, 0))] * 2,
        out_specs=[pl.BlockSpec((1, part, width), lambda i, j: (i, j, 0))] * X,
        out_shape=[jax.ShapeDtypeStruct(shape[1:], jnp.bfloat16)] * X,
        compiler_params=pltpu.CompilerParams(vmem_limit_bytes=GRANT),
        cost_estimate=pl.CostEstimate(
            flops=rows * block_len * width,
            bytes_accessed=6 * rows * block_len * width,
            transcendentals=0,
        ),
    )(kept.reshape(shape), arrived.reshape(shape))


def finish_kernel(parts, width, degree, bias, own, own_corrupt, *refs):
    ins, (clean, corrupt, hidden, spread) = refs[:-4], refs[-4:]
    for at in range(len(ins) // (parts + 1)):
        group = ins[at * (parts + 1) : (at + 1) * (parts + 1)]
        total = group[parts][...].astype(jnp.float32)
        for ref in group[:parts]:
            total += ref[0].astype(jnp.float32)
        columns = slice(at * width, (at + 1) * width)
        inner = slice(0, width)
        for out, value, source in (
            (clean, total[:, :width], own[:, columns]),
            (corrupt, total[:, width:], own_corrupt[at][:, inner]),
        ):
            value = value + source.astype(jnp.float32) / degree[...] + bias[:, columns]
            out[:, columns] = jnp.maximum(value, 0.0)
    final = clean[...]
    hidden[...] = final.astype(hidden.dtype)
    sums = jnp.sum(final, axis=0, keepdims=True).astype(spread.dtype)
    spread[...] = jnp.broadcast_to(sums, spread.shape)


def finish(devices, degree, bias, own, own_corrupt, groups):
    block_len, hidden = own.shape
    width = hidden // len(groups)
    parts = len(groups[0]) - 1
    near = pl.BlockSpec((1, block_len, 2 * width), lambda i: (0, 0, 0))
    last = pl.BlockSpec((block_len, 2 * width), lambda i: (0, 0))

    def whole(*shape):
        return pl.BlockSpec(shape, lambda i: (0,) * len(shape))

    return pl.pallas_call(
        functools.partial(finish_kernel, parts, width),
        grid=(1,),
        in_specs=[
            whole(block_len, 1),
            whole(1, hidden),
            whole(block_len, hidden),
            whole(len(groups), block_len, width),
        ]
        + ([near] * parts + [last]) * len(groups),
        out_specs=[whole(block_len, hidden)] * 3 + [whole(devices, hidden)],
        out_shape=[
            jax.ShapeDtypeStruct((block_len, hidden), jnp.float32),
            jax.ShapeDtypeStruct((block_len, hidden), jnp.float32),
            jax.ShapeDtypeStruct((block_len, hidden), jnp.bfloat16),
            jax.ShapeDtypeStruct((devices, hidden), jnp.bfloat16),
        ],
        compiler_params=pltpu.CompilerParams(vmem_limit_bytes=GRANT),
    )(degree, bias, own, own_corrupt, *[value for group in groups for value in group])


def score_kernel(nodes, gathered, disc_weight, clean, corrupt, scores, spread):
    column_total = jnp.sum(gathered[...].astype(jnp.float32), axis=0, keepdims=True)
    summary = jax.nn.sigmoid(column_total / nodes)
    lanes = (((1,), (1,)), ((), ()))
    exact = dict(precision=lax.Precision.HIGHEST, preferred_element_type=jnp.float32)
    summary = jnp.broadcast_to(summary, (8, summary.shape[1]))
    probe = lax.dot_general(summary, disc_weight[...], lanes, **exact)
    clean_score = lax.dot_general(probe, clean[...], lanes, **exact)[:1]
    corrupt_score = lax.dot_general(probe, corrupt[...], lanes, **exact)[:1]
    scores[0:1] = clean_score
    scores[1:2] = corrupt_score

    def softplus(value):
        return jnp.maximum(value, 0.0) + jnp.log1p(jnp.exp(-jnp.abs(value)))

    terms = softplus(-clean_score) + softplus(corrupt_score)
    spread[...] = jnp.broadcast_to(jnp.sum(terms, axis=1, keepdims=True), spread.shape)


def score(nodes, devices, gathered, disc_weight, clean, corrupt):
    block_len = clean.shape[0]
    return pl.pallas_call(
        functools.partial(score_kernel, nodes),
        out_shape=[
            jax.ShapeDtypeStruct((2, block_len), jnp.float32),
            jax.ShapeDtypeStruct((devices, 128), jnp.float32),
        ],
        compiler_params=pltpu.CompilerParams(vmem_limit_bytes=GRANT),
    )(gathered, disc_weight, clean, corrupt)


def step(
    features,
    proj_weight,
    bias,
    disc_weight,
    adjacency,
    row_block,
    col_block,
    block_count,
    degree,
    corrupt_source,
):
    block_len = adjacency.shape[-1]
    hidden = proj_weight.shape[1]
    wide_size = lax.axis_size("wide")
    narrow_size = lax.axis_size("narrow")
    devices = wide_size * narrow_size
    wide_at = lax.axis_index("wide")
    narrow_at = lax.axis_index("narrow")
    y, zh = wide_at // ZH, wide_at % ZH
    x, zl, core = narrow_at // (ZL * CORES), narrow_at // CORES % ZL, narrow_at % CORES
    chunks = 2
    width = hidden // chunks

    own = []
    panels = []
    for h in range(chunks):
        weight = proj_weight[:, h * width : (h + 1) * width]
        part = jnp.dot(features, weight, preferred_element_type=jnp.float32)
        part = part.astype(jnp.bfloat16)
        own.append(part)
        along_z = [part] + [to_wide(part, dz=k) for k in range(1, ZH)]
        along_z = jnp.stack(along_z)
        panels.append([along_z] + [to_wide(along_z, dy=k) for k in range(1, Y)])

    inv_root = lax.rsqrt(degree.astype(jnp.float32))
    col_roots = lax.dynamic_index_in_dim(
        inv_root.reshape(wide_size, narrow_size, block_len), narrow_at, 1, keepdims=False
    )
    row_roots = lax.dynamic_index_in_dim(
        inv_root.reshape(wide_size, narrow_size, block_len), wide_at, 0, keepdims=False
    )
    slot_rows = row_block[0, 0]
    slot_cols = col_block[0, 0]
    normed = (
        adjacency[0, 0].astype(jnp.float32)
        * row_roots[slot_rows][:, :, None]
        * col_roots[slot_cols][:, None, :]
    ).astype(jnp.bfloat16)

    slot_ids = jnp.arange(SLOTS, dtype=jnp.int32)
    keys = jnp.where(slot_ids < block_count[0, 0], slot_rows, narrow_size)
    before = (keys[None, :] < keys[:, None]) | (
        (keys[None, :] == keys[:, None]) & (slot_ids[None, :] < slot_ids[:, None])
    )
    rank = jnp.sum(before.astype(jnp.int32), axis=1)
    order = jnp.sum(jnp.where(rank[None, :] == slot_ids[:, None], slot_ids[None, :], 0), axis=1)
    starts = jnp.sum(
        (keys[None, :] < jnp.arange(narrow_size + 1, dtype=jnp.int32)[:, None]).astype(jnp.int32),
        axis=1,
    )
    columns = jnp.arange(wide_size, dtype=jnp.int32)
    sources = (
        lax.dynamic_index_in_dim(
            corrupt_source.reshape(wide_size, narrow_size), narrow_at, 1, keepdims=False
        )
        // narrow_size
    )
    slot_sources = jnp.sum(
        jnp.where(slot_cols[:, None] == columns[None, :], sources[None, :], 0), axis=1
    )
    own_source = jnp.sum(jnp.where(columns == wide_at, sources, 0))
    steps_x = jnp.arange(X, dtype=jnp.int32)
    flips = jnp.arange(ZL, dtype=jnp.int32)
    targets = ((x + steps_x)[:, None] % X * ZL + (zl ^ flips)[None, :]) * CORES
    dest = (y - jnp.arange(Y, dtype=jnp.int32))[:, None] % Y * ZH + (
        zh - jnp.arange(ZH, dtype=jnp.int32)
    )[None, :] % ZH
    parts = [
        order,
        slot_cols,
        slot_sources,
        starts,
        (targets + 1 - core).reshape(-1),
        (targets + core).reshape(-1),
        dest.reshape(-1),
        own_source[None],
    ]
    parts.append(jnp.zeros((META - sum(part.shape[0] for part in parts),), jnp.int32))
    meta = jnp.concatenate([part.astype(jnp.int32) for part in parts])

    own_corrupt = []
    groups = []
    for h in range(chunks):
        sent, kept, own_part = spmm(meta, normed, panels[h])
        own_corrupt.append(own_part)
        arrived = to_narrow(sent, flip_core=1)
        halves = pair_sum(kept, arrived)
        got = [halves[0]] + [to_narrow(halves[k], dx=k) for k in range(1, X)]
        far = sum(value[1].astype(jnp.float32) for value in got).astype(jnp.bfloat16)
        last = to_narrow(far, flip_z=1)
        groups.append(got + [last])

    own_degree = lax.dynamic_index_in_dim(
        degree.reshape(devices, block_len), wide_at * narrow_size + narrow_at, 0, keepdims=False
    )
    degree_float = own_degree.astype(jnp.float32)[:, None]
    nodes = block_len * devices
    clean_h, corrupt_h, hidden_out, spread = finish(
        devices,
        degree_float,
        bias[None, :],
        jnp.concatenate(own, axis=1),
        jnp.stack(own_corrupt),
        groups,
    )
    gathered = lax.all_to_all(spread, BOTH, 0, 0, tiled=True)
    scores, spread = score(nodes, devices, gathered, disc_weight, clean_h, corrupt_h)
    gathered = lax.all_to_all(spread, BOTH, 0, 0, tiled=True)
    loss = jnp.sum(gathered[:, 0]) / (2 * nodes)
    return (hidden_out, scores, loss)


def solution(mesh):
    placed = (
        P(("wide", "narrow"), None),
        P(),
        P(),
        P(),
        P("wide", "narrow", None, None, None),
        P("wide", "narrow", None),
        P("wide", "narrow", None),
        P("wide", "narrow"),
        P(),
        P(),
    )
    return jax.shard_map(
        step,
        mesh=mesh,
        in_specs=placed,
        out_specs=(P(("wide", "narrow"), None), P(None, ("wide", "narrow")), P()),
        check_vma=False,
    )
```

profile of v0, /device:TPU:1, one launch (start us, length us, event | category | flops | bytes accessed | tf_op | source)
XLA Modules:
  0.0 218.8 jit_solution(14282831580190358395)
XLA Ops:
  2.9 3.9 %collective-permute-start.6 = (bf16[256,256]{1,0:T(8,128)(2,1)S(1)}, bf16[256,256]{1,0:T(8,128)(2,1)S(1)}, u32[]{:S(2)}, u32[]{:S(2)}) collective-permute-start(bf16[256,256]{1,0:T(8,128)(2,1)S(1)} %convolution_convert_fusion), channel_id=1, source_target_pairs={{0,16},{16,32},{32,48},{48,0},{64,80},{80,96},{96,112},{112,64},{1... | collective-permute-start | bytes 393224 | tf_op jit(solution)/shard_map/ppermute | solution.py:37
  6.8 5.1 %collective-permute-start.7 = (bf16[256,256]{1,0:T(8,128)(2,1)S(1)}, bf16[256,256]{1,0:T(8,128)(2,1)S(1)}, u32[]{:S(2)}, u32[]{:S(2)}) collective-permute-start(bf16[256,256]{1,0:T(8,128)(2,1)S(1)} %convolution_convert_fusion), channel_id=1, source_target_pairs={{0,32},{16,48},{32,0},{48,16},{64,96},{80,112},{96,64},{112,80},{1... | collective-permute-start | bytes 393224 | tf_op jit(solution)/shard_map/ppermute | solution.py:37
  11.9 2.4 %collective-permute-start.8 = (bf16[256,256]{1,0:T(8,128)(2,1)S(1)}, bf16[256,256]{1,0:T(8,128)(2,1)S(1)}, u32[]{:S(2)}, u32[]{:S(2)}) collective-permute-start(bf16[256,256]{1,0:T(8,128)(2,1)S(1)} %convolution_convert_fusion), channel_id=1, source_target_pairs={{0,48},{16,0},{32,16},{48,32},{64,112},{80,64},{96,80},{112,96},{1... | collective-permute-start | bytes 393224 | tf_op jit(solution)/shard_map/ppermute | solution.py:37
  22.6 4.5 %fusion.1.normed = bf16[24,256,256]{2,1,0:T(8,128)(2,1)} fusion(s32[1,1,24,256,256]{4,3,2,1,0:T(8,128)} %param.14, f32[24,256]{1,0:T(8,128)S(1)} %gather_fusion.1, f32[24,256]{1,0:T(8,128)S(1)} %gather_fusion), kind=kLoop, calls=%fused_computation.4 | loop fusion | flops 6291456 | bytes 9486336 | tf_op jit(solution)/shard_map/convert_element_type | solution.py:296
  27.1 3.4 %collective-permute-done.8 = bf16[256,256]{1,0:T(8,128)(2,1)S(1)} collective-permute-done((bf16[256,256]{1,0:T(8,128)(2,1)S(1)}, bf16[256,256]{1,0:T(8,128)(2,1)S(1)}, u32[]{:S(2)}, u32[]{:S(2)}) %collective-permute-start.8) | collective-permute-done | bytes 131104 | tf_op jit(solution)/shard_map/ppermute | solution.py:37
  30.5 3.0 %collective-permute-start.10 = (bf16[4,256,256]{2,1,0:T(8,128)(2,1)S(1)}, bf16[4,256,256]{2,1,0:T(8,128)(2,1)S(1)}, u32[]{:S(2)}, u32[]{:S(2)}) collective-permute-start(bf16[4,256,256]{2,1,0:T(8,128)(2,1)S(1)} %pad_maximum_fusion.1.refs_0_), channel_id=1, source_target_pairs={{0,128},{16,144},{32,160},{48,176},{64,192},{80,208},{96,224},{112... | collective-permute-start | bytes 1572872 | tf_op jit(solution)/shard_map/ppermute | solution.py:37
  35.3 3.4 %collective-permute-start.2 = (bf16[256,256]{1,0:T(8,128)(2,1)S(1)}, bf16[256,256]{1,0:T(8,128)(2,1)S(1)}, u32[]{:S(2)}, u32[]{:S(2)}) collective-permute-start(bf16[256,256]{1,0:T(8,128)(2,1)S(1)} %convolution_convert_fusion.1), channel_id=1, source_target_pairs={{0,48},{16,0},{32,16},{48,32},{64,112},{80,64},{96,80},{112,96},{1... | collective-permute-start | bytes 393224 | tf_op jit(solution)/shard_map/ppermute | solution.py:37
  39.2 3.8 %collective-permute-done.2 = bf16[256,256]{1,0:T(8,128)(2,1)S(1)} collective-permute-done((bf16[256,256]{1,0:T(8,128)(2,1)S(1)}, bf16[256,256]{1,0:T(8,128)(2,1)S(1)}, u32[]{:S(2)}, u32[]{:S(2)}) %collective-permute-start.2) | collective-permute-done | bytes 131104 | tf_op jit(solution)/shard_map/ppermute | solution.py:37
  43.7 2.5 %collective-permute-start.4 = (bf16[4,256,256]{2,1,0:T(8,128)(2,1)S(1)}, bf16[4,256,256]{2,1,0:T(8,128)(2,1)}, u32[]{:S(2)}, u32[]{:S(2)}) collective-permute-start(bf16[4,256,256]{2,1,0:T(8,128)(2,1)S(1)} %pad_maximum_fusion.refs_0_), channel_id=1, source_target_pairs={{0,128},{16,144},{32,160},{48,176},{64,192},{80,208},{96,224},{112... | collective-permute-start | bytes 1572872 | tf_op jit(solution)/shard_map/ppermute | solution.py:37
  49.1 7.7 %collective-permute-done.11.refs_3_ = bf16[4,256,256]{2,1,0:T(8,128)(2,1)S(1)} collective-permute-done((bf16[4,256,256]{2,1,0:T(8,128)(2,1)S(1)}, bf16[4,256,256]{2,1,0:T(8,128)(2,1)S(1)}, u32[]{:S(2)}, u32[]{:S(2)}) %collective-permute-start.11) | collective-permute-done | bytes 524320 | tf_op jit(solution)/shard_map/ppermute | solution.py:37
  57.6 12.8 %shard_map.122 = (bf16[8,256,512]{2,1,0:T(8,128)(2,1)}, bf16[8,256,512]{2,1,0:T(8,128)(2,1)}, bf16[256,256]{1,0:T(8,128)(2,1)}) custom-call(s32[128]{0:T(128)} %concatenate.7.meta, bf16[24,256,256]{2,1,0:T(8,128)(2,1)} %fusion.1.normed, bf16[4,256,256]{2,1,0:T(8,128)(2,1)} %copy-done.8, bf16[4,256,256]{2,1,0:T(8,128)(2,1)} %collective-permute-done.9.refs_1_, ...), custom_call_target="tpu_custom_call" | custom-call | flops 1610612736 | bytes 10485760 | tf_op jit(solution)/shard_map/pallas_call | solution.py:114
  71.1 7.9 %collective-permute-done.4.refs_2_ = bf16[4,256,256]{2,1,0:T(8,128)(2,1)} collective-permute-done((bf16[4,256,256]{2,1,0:T(8,128)(2,1)S(1)}, bf16[4,256,256]{2,1,0:T(8,128)(2,1)}, u32[]{:S(2)}, u32[]{:S(2)}) %collective-permute-start.4) | collective-permute-done | bytes 524320 | tf_op jit(solution)/shard_map/ppermute | solution.py:37
  79.4 12.9 %shard_map.121 = (bf16[8,256,512]{2,1,0:T(8,128)(2,1)}, bf16[8,256,512]{2,1,0:T(8,128)(2,1)}, bf16[256,256]{1,0:T(8,128)(2,1)}) custom-call(s32[128]{0:T(128)} %concatenate.7.meta, bf16[24,256,256]{2,1,0:T(8,128)(2,1)} %fusion.1.normed, bf16[4,256,256]{2,1,0:T(8,128)(2,1)} %copy-done.9, bf16[4,256,256]{2,1,0:T(8,128)(2,1)} %collective-permute-done.3.refs_1_, ...), custom_call_target="tpu_custom_call" | custom-call | flops 1610612736 | bytes 10485760 | tf_op jit(solution)/shard_map/pallas_call | solution.py:114
  93.7 4.2 %shard_map.124 = (bf16[2,256,512]{2,1,0:T(8,128)(2,1)}, bf16[2,256,512]{2,1,0:T(8,128)(2,1)}, bf16[2,256,512]{2,1,0:T(8,128)(2,1)}, bf16[2,256,512]{2,1,0:T(8,128)(2,1)}) custom-call(bf16[4,2,256,512]{3,2,1,0:T(8,128)(2,1)} %bitcast.58, bf16[4,2,256,512]{3,2,1,0:T(8,128)(2,1)} %bitcast.59), custom_call_target="tpu_custom_call" | custom-call | flops 1048576 | bytes 6291456 | tf_op jit(solution)/shard_map/pallas_call | solution.py:150
  99.0 2.6 %collective-permute-start.19 = (bf16[2,256,512]{2,1,0:T(8,128)(2,1)}, bf16[2,256,512]{2,1,0:T(8,128)(2,1)S(1)}, u32[]{:S(2)}, u32[]{:S(2)}) collective-permute-start(bf16[2,256,512]{2,1,0:T(8,128)(2,1)} %get-tuple-element.35), channel_id=1, source_target_pairs={{0,8},{1,9},{2,10},{3,11},{4,12},{5,13},{6,14},{7,15},{8,0},{9,1},... | collective-permute-start | bytes 1572872 | tf_op jit(solution)/shard_map/ppermute | solution.py:33
  101.6 4.2 %shard_map.123 = (bf16[2,256,512]{2,1,0:T(8,128)(2,1)}, bf16[2,256,512]{2,1,0:T(8,128)(2,1)}, bf16[2,256,512]{2,1,0:T(8,128)(2,1)}, bf16[2,256,512]{2,1,0:T(8,128)(2,1)}) custom-call(bf16[4,2,256,512]{3,2,1,0:T(8,128)(2,1)} %bitcast.57, bf16[4,2,256,512]{3,2,1,0:T(8,128)(2,1)} %bitcast.23.arrived), custom_call_target="tpu_custom_call" | custom-call | flops 1048576 | bytes 6291456 | tf_op jit(solution)/shard_map/pallas_call | solution.py:150
  107.7 4.7 %collective-permute-done.18.refs_6_ = bf16[2,256,512]{2,1,0:T(8,128)(2,1)S(1)} collective-permute-done((bf16[2,256,512]{2,1,0:T(8,128)(2,1)}, bf16[2,256,512]{2,1,0:T(8,128)(2,1)S(1)}, u32[]{:S(2)}, u32[]{:S(2)}) %collective-permute-start.18) | collective-permute-done | bytes 524320 | tf_op jit(solution)/shard_map/ppermute | solution.py:33
  115.8 9.3 %collective-permute-done.19.refs_7_ = bf16[2,256,512]{2,1,0:T(8,128)(2,1)S(1)} collective-permute-done((bf16[2,256,512]{2,1,0:T(8,128)(2,1)}, bf16[2,256,512]{2,1,0:T(8,128)(2,1)S(1)}, u32[]{:S(2)}, u32[]{:S(2)}) %collective-permute-start.19) | collective-permute-done | bytes 524320 | tf_op jit(solution)/shard_map/ppermute | solution.py:33
  126.1 8.8 %collective-permute-done.13.refs_1_ = bf16[2,256,512]{2,1,0:T(8,128)(2,1)S(1)} collective-permute-done((bf16[2,256,512]{2,1,0:T(8,128)(2,1)}, bf16[2,256,512]{2,1,0:T(8,128)(2,1)S(1)}, u32[]{:S(2)}, u32[]{:S(2)}) %collective-permute-start.13) | collective-permute-done | bytes 524320 | tf_op jit(solution)/shard_map/ppermute | solution.py:33
  134.9 12.7 %collective-permute-done.14.refs_2_ = bf16[2,256,512]{2,1,0:T(8,128)(2,1)S(1)} collective-permute-done((bf16[2,256,512]{2,1,0:T(8,128)(2,1)}, bf16[2,256,512]{2,1,0:T(8,128)(2,1)S(1)}, u32[]{:S(2)}, u32[]{:S(2)}) %collective-permute-start.14) | collective-permute-done | bytes 524320 | tf_op jit(solution)/shard_map/ppermute | solution.py:33
  157.6 3.4 %shard_map.125 = (f32[256,512]{1,0:T(8,128)}, f32[256,512]{1,0:T(8,128)}, bf16[256,512]{1,0:T(8,128)(2,1)}, bf16[256,512]{1,0:T(8,128)(2,1)}) custom-call(f32[256,1]{1,0:T(8,128)} %copy.33.degree, f32[1,512]{1,0:T(1,128)} %bitcast.74, bf16[256,512]{1,0:T(8,128)(2,1)} %pad_maximum_fusion.2.own, bf16[2,256,256]{2,1,0:T(8,128)(2,1)} %pad_maximum_fusion.3.own_corrupt, ...), custom_call_target="tpu_custom_call" | custom-call | tf_op jit(solution)/shard_map/pallas_call | solution.py:196
  163.3 28.9 %all_to_all.23 = bf16[256,2,256]{2,1,0:T(2,128)(2,1)S(1)} all-to-all(bf16[256,2,256]{2,1,0:T(2,128)(2,1)S(1)} %reshape.280), channel_id=1, replica_groups=mesh['wide'=16,'narrow'=16] {'wide','narrow'}, dimensions={0} | all-to-all | bytes 524288 | tf_op jit(solution)/shard_map/all_to_all | solution.py:364
  193.2 4.2 %shard_map.126 = (f32[2,256]{1,0:T(2,128)}, f32[256,128]{1,0:T(8,128)}) custom-call(bf16[256,512]{1,0:T(8,128)(2,1)} %bitcast.60, f32[512,512]{1,0:T(8,128)} %disc_weight.1, f32[256,512]{1,0:T(8,128)} %get-tuple-element.39.clean, f32[256,512]{1,0:T(8,128)} %get-tuple-element.40.corrupt), custom_call_target="tpu_custom_call" | custom-call | tf_op jit(solution)/shard_map/pallas_call | solution.py:238
  197.3 19.1 %all_to_all.24 = f32[256,1,128]{2,1,0:T(1,128)S(1)} all-to-all(f32[256,1,128]{2,1,0:T(1,128)} %bitcast.65), channel_id=1, replica_groups=mesh['wide'=16,'narrow'=16] {'wide','narrow'}, dimensions={0} | all-to-all | bytes 262144 | tf_op jit(solution)/shard_map/all_to_all | solution.py:366
  (110 shorter events, 40.1 us)
Async XLA Ops:
  2.9 24.1 %collective-permute-start.6 = (bf16[256,256]{1,0:T(8,128)(2,1)S(1)}, bf16[256,256]{1,0:T(8,128)(2,1)S(1)}, u32[]{:S(2)}, u32[]{:S(2)}) collective-permute-start(bf16[256,256]{1,0:T(8,128)(2,1)S(1)} %convolution_convert_fusion), channel_id=1, source_target_pairs={{0,16},{16,32},{32,48},{48,0},{64,80},{80,96},{96,112},{112,64},{1... | collective-permute-start | bytes 393224 | tf_op jit(solution)/shard_map/ppermute | solution.py:37
  6.8 20.3 %collective-permute-start.7 = (bf16[256,256]{1,0:T(8,128)(2,1)S(1)}, bf16[256,256]{1,0:T(8,128)(2,1)S(1)}, u32[]{:S(2)}, u32[]{:S(2)}) collective-permute-start(bf16[256,256]{1,0:T(8,128)(2,1)S(1)} %convolution_convert_fusion), channel_id=1, source_target_pairs={{0,32},{16,48},{32,0},{48,16},{64,96},{80,112},{96,64},{112,80},{1... | collective-permute-start | bytes 393224 | tf_op jit(solution)/shard_map/ppermute | solution.py:37
  11.9 18.6 %collective-permute-start.8 = (bf16[256,256]{1,0:T(8,128)(2,1)S(1)}, bf16[256,256]{1,0:T(8,128)(2,1)S(1)}, u32[]{:S(2)}, u32[]{:S(2)}) collective-permute-start(bf16[256,256]{1,0:T(8,128)(2,1)S(1)} %convolution_convert_fusion), channel_id=1, source_target_pairs={{0,48},{16,0},{32,16},{48,32},{64,112},{80,64},{96,80},{112,96},{1... | collective-permute-start | bytes 393224 | tf_op jit(solution)/shard_map/ppermute | solution.py:37
  15.6 54.9 %copy-start.11 = (bf16[256,256]{1,0:T(8,128)(2,1)}, bf16[256,256]{1,0:T(8,128)(2,1)S(1)}, u32[]{:S(2)}) copy-start(bf16[256,256]{1,0:T(8,128)(2,1)S(1)} %convolution_convert_fusion.1) | copy-start | bytes 393220
  15.6 19.7 %collective-permute-start = (bf16[256,256]{1,0:T(8,128)(2,1)S(1)}, bf16[256,256]{1,0:T(8,128)(2,1)S(1)}, u32[]{:S(2)}, u32[]{:S(2)}) collective-permute-start(bf16[256,256]{1,0:T(8,128)(2,1)S(1)} %convolution_convert_fusion.1), channel_id=1, source_target_pairs={{0,16},{16,32},{32,48},{48,0},{64,80},{80,96},{96,112},{112,64},{1... | collective-permute-start | bytes 393224 | tf_op jit(solution)/shard_map/ppermute | solution.py:37
  15.7 23.5 %collective-permute-start.1 = (bf16[256,256]{1,0:T(8,128)(2,1)S(1)}, bf16[256,256]{1,0:T(8,128)(2,1)S(1)}, u32[]{:S(2)}, u32[]{:S(2)}) collective-permute-start(bf16[256,256]{1,0:T(8,128)(2,1)S(1)} %convolution_convert_fusion.1), channel_id=1, source_target_pairs={{0,32},{16,48},{32,0},{48,16},{64,96},{80,112},{96,64},{112,80},{1... | collective-permute-start | bytes 393224 | tf_op jit(solution)/shard_map/ppermute | solution.py:37
  30.5 15.6 %collective-permute-start.10 = (bf16[4,256,256]{2,1,0:T(8,128)(2,1)S(1)}, bf16[4,256,256]{2,1,0:T(8,128)(2,1)S(1)}, u32[]{:S(2)}, u32[]{:S(2)}) collective-permute-start(bf16[4,256,256]{2,1,0:T(8,128)(2,1)S(1)} %pad_maximum_fusion.1.refs_0_), channel_id=1, source_target_pairs={{0,128},{16,144},{32,160},{48,176},{64,192},{80,208},{96,224},{112... | collective-permute-start | bytes 1572872 | tf_op jit(solution)/shard_map/ppermute | solution.py:37
  33.5 23.3 %collective-permute-start.11 = (bf16[4,256,256]{2,1,0:T(8,128)(2,1)S(1)}, bf16[4,256,256]{2,1,0:T(8,128)(2,1)S(1)}, u32[]{:S(2)}, u32[]{:S(2)}) collective-permute-start(bf16[4,256,256]{2,1,0:T(8,128)(2,1)S(1)} %pad_maximum_fusion.1.refs_0_), channel_id=1, source_target_pairs={{0,192},{16,208},{32,224},{48,240},{64,0},{80,16},{96,32},{112,48}... | collective-permute-start | bytes 1572872 | tf_op jit(solution)/shard_map/ppermute | solution.py:37
  34.3 23.0 %collective-permute-start.9 = (bf16[4,256,256]{2,1,0:T(8,128)(2,1)S(1)}, bf16[4,256,256]{2,1,0:T(8,128)(2,1)}, u32[]{:S(2)}, u32[]{:S(2)}) collective-permute-start(bf16[4,256,256]{2,1,0:T(8,128)(2,1)S(1)} %pad_maximum_fusion.1.refs_0_), channel_id=1, source_target_pairs={{0,64},{16,80},{32,96},{48,112},{64,128},{80,144},{96,160},{112,17... | collective-permute-start | bytes 1572872 | tf_op jit(solution)/shard_map/ppermute | solution.py:37
  35.3 7.6 %collective-permute-start.2 = (bf16[256,256]{1,0:T(8,128)(2,1)S(1)}, bf16[256,256]{1,0:T(8,128)(2,1)S(1)}, u32[]{:S(2)}, u32[]{:S(2)}) collective-permute-start(bf16[256,256]{1,0:T(8,128)(2,1)S(1)} %convolution_convert_fusion.1), channel_id=1, source_target_pairs={{0,48},{16,0},{32,16},{48,32},{64,112},{80,64},{96,80},{112,96},{1... | collective-permute-start | bytes 393224 | tf_op jit(solution)/shard_map/ppermute | solution.py:37
  43.0 28.1 %collective-permute-start.3 = (bf16[4,256,256]{2,1,0:T(8,128)(2,1)S(1)}, bf16[4,256,256]{2,1,0:T(8,128)(2,1)}, u32[]{:S(2)}, u32[]{:S(2)}) collective-permute-start(bf16[4,256,256]{2,1,0:T(8,128)(2,1)S(1)} %pad_maximum_fusion.refs_0_), channel_id=1, source_target_pairs={{0,64},{16,80},{32,96},{48,112},{64,128},{80,144},{96,160},{112,17... | collective-permute-start | bytes 1572872 | tf_op jit(solution)/shard_map/ppermute | solution.py:37
  43.7 35.3 %collective-permute-start.4 = (bf16[4,256,256]{2,1,0:T(8,128)(2,1)S(1)}, bf16[4,256,256]{2,1,0:T(8,128)(2,1)}, u32[]{:S(2)}, u32[]{:S(2)}) collective-permute-start(bf16[4,256,256]{2,1,0:T(8,128)(2,1)S(1)} %pad_maximum_fusion.refs_0_), channel_id=1, source_target_pairs={{0,128},{16,144},{32,160},{48,176},{64,192},{80,208},{96,224},{112... | collective-permute-start | bytes 1572872 | tf_op jit(solution)/shard_map/ppermute | solution.py:37
  46.2 33.2 %collective-permute-start.5 = (bf16[4,256,256]{2,1,0:T(8,128)(2,1)S(1)}, bf16[4,256,256]{2,1,0:T(8,128)(2,1)}, u32[]{:S(2)}, u32[]{:S(2)}) collective-permute-start(bf16[4,256,256]{2,1,0:T(8,128)(2,1)S(1)} %pad_maximum_fusion.refs_0_), channel_id=1, source_target_pairs={{0,192},{16,208},{32,224},{48,240},{64,0},{80,16},{96,32},{112,48}... | collective-permute-start | bytes 1572872 | tf_op jit(solution)/shard_map/ppermute | solution.py:37
  70.5 21.9 %collective-permute-start.17 = (bf16[8,256,512]{2,1,0:T(8,128)(2,1)}, bf16[8,256,512]{2,1,0:T(8,128)(2,1)S(1)}, u32[]{:S(2)}, u32[]{:S(2)}) collective-permute-start(bf16[8,256,512]{2,1,0:T(8,128)(2,1)} %get-tuple-element.32), channel_id=1, source_target_pairs={{0,1},{1,0},{2,3},{3,2},{4,5},{5,4},{6,7},{7,6},{8,9},{9,8},{10,11... | collective-permute-start | bytes 6291464 | tf_op jit(solution)/shard_map/ppermute | solution.py:33
  92.3 9.3 %collective-permute-start.12 = (bf16[8,256,512]{2,1,0:T(8,128)(2,1)}, bf16[8,256,512]{2,1,0:T(8,128)(2,1)}, u32[]{:S(2)}, u32[]{:S(2)}) collective-permute-start(bf16[8,256,512]{2,1,0:T(8,128)(2,1)} %get-tuple-element.26), channel_id=1, source_target_pairs={{0,1},{1,0},{2,3},{3,2},{4,5},{5,4},{6,7},{7,6},{8,9},{9,8},{10,11... | collective-permute-start | bytes 6291464 | tf_op jit(solution)/shard_map/ppermute | solution.py:33
  97.9 14.5 %collective-permute-start.18 = (bf16[2,256,512]{2,1,0:T(8,128)(2,1)}, bf16[2,256,512]{2,1,0:T(8,128)(2,1)S(1)}, u32[]{:S(2)}, u32[]{:S(2)}) collective-permute-start(bf16[2,256,512]{2,1,0:T(8,128)(2,1)} %get-tuple-element.34), channel_id=1, source_target_pairs={{0,4},{1,5},{2,6},{3,7},{4,8},{5,9},{6,10},{7,11},{8,12},{9,13},{1... | collective-permute-start | bytes 1572872 | tf_op jit(solution)/shard_map/ppermute | solution.py:33
  99.0 26.1 %collective-permute-start.19 = (bf16[2,256,512]{2,1,0:T(8,128)(2,1)}, bf16[2,256,512]{2,1,0:T(8,128)(2,1)S(1)}, u32[]{:S(2)}, u32[]{:S(2)}) collective-permute-start(bf16[2,256,512]{2,1,0:T(8,128)(2,1)} %get-tuple-element.35), channel_id=1, source_target_pairs={{0,8},{1,9},{2,10},{3,11},{4,12},{5,13},{6,14},{7,15},{8,0},{9,1},... | collective-permute-start | bytes 1572872 | tf_op jit(solution)/shard_map/ppermute | solution.py:33
  101.6 23.5 %collective-permute-start.20 = (bf16[2,256,512]{2,1,0:T(8,128)(2,1)}, bf16[2,256,512]{2,1,0:T(8,128)(2,1)S(1)}, u32[]{:S(2)}, u32[]{:S(2)}) collective-permute-start(bf16[2,256,512]{2,1,0:T(8,128)(2,1)} %get-tuple-element.36), channel_id=1, source_target_pairs={{0,12},{1,13},{2,14},{3,15},{4,0},{5,1},{6,2},{7,3},{8,4},{9,5},{1... | collective-permute-start | bytes 1572872 | tf_op jit(solution)/shard_map/ppermute | solution.py:33
  105.8 29.0 %collective-permute-start.13 = (bf16[2,256,512]{2,1,0:T(8,128)(2,1)}, bf16[2,256,512]{2,1,0:T(8,128)(2,1)S(1)}, u32[]{:S(2)}, u32[]{:S(2)}) collective-permute-start(bf16[2,256,512]{2,1,0:T(8,128)(2,1)} %get-tuple-element.28), channel_id=1, source_target_pairs={{0,4},{1,5},{2,6},{3,7},{4,8},{5,9},{6,10},{7,11},{8,12},{9,13},{1... | collective-permute-start | bytes 1572872 | tf_op jit(solution)/shard_map/ppermute | solution.py:33
  107.3 40.3 %collective-permute-start.14 = (bf16[2,256,512]{2,1,0:T(8,128)(2,1)}, bf16[2,256,512]{2,1,0:T(8,128)(2,1)S(1)}, u32[]{:S(2)}, u32[]{:S(2)}) collective-permute-start(bf16[2,256,512]{2,1,0:T(8,128)(2,1)} %get-tuple-element.29), channel_id=1, source_target_pairs={{0,8},{1,9},{2,10},{3,11},{4,12},{5,13},{6,14},{7,15},{8,0},{9,1},... | collective-permute-start | bytes 1572872 | tf_op jit(solution)/shard_map/ppermute | solution.py:33
  112.4 44.4 %copy-start.3 = (bf16[2,256,512]{2,1,0:T(8,128)(2,1)}, bf16[2,256,512]{2,1,0:T(8,128)(2,1)S(1)}, u32[]{:S(2)}) copy-start(bf16[2,256,512]{2,1,0:T(8,128)(2,1)S(1)} %collective-permute-done.18.refs_6_) | copy-start | bytes 1572868
  112.4 35.2 %collective-permute-start.15 = (bf16[2,256,512]{2,1,0:T(8,128)(2,1)}, bf16[2,256,512]{2,1,0:T(8,128)(2,1)}, u32[]{:S(2)}, u32[]{:S(2)}) collective-permute-start(bf16[2,256,512]{2,1,0:T(8,128)(2,1)} %get-tuple-element.30), channel_id=1, source_target_pairs={{0,12},{1,13},{2,14},{3,15},{4,0},{5,1},{6,2},{7,3},{8,4},{9,5},{1... | collective-permute-start | bytes 1572872 | tf_op jit(solution)/shard_map/ppermute | solution.py:33
  126.1 28.5 %collective-permute-start.21 = (bf16[256,512]{1,0:T(8,128)(2,1)}, bf16[256,512]{1,0:T(8,128)(2,1)S(1)}, u32[]{:S(2)}, u32[]{:S(2)}) collective-permute-start(bf16[256,512]{1,0:T(8,128)(2,1)} %fusion.5), channel_id=1, source_target_pairs={{0,2},{1,3},{2,0},{3,1},{4,6},{5,7},{6,4},{7,5},{8,10},{9,11},{10,... | collective-permute-start | bytes 786440 | tf_op jit(solution)/shard_map/ppermute | solution.py:33
  149.7 7.2 %collective-permute-start.16 = (bf16[256,512]{1,0:T(8,128)(2,1)}, bf16[256,512]{1,0:T(8,128)(2,1)S(1)}, u32[]{:S(2)}, u32[]{:S(2)}) collective-permute-start(bf16[256,512]{1,0:T(8,128)(2,1)} %fusion.4), channel_id=1, source_target_pairs={{0,2},{1,3},{2,0},{3,1},{4,6},{5,7},{6,4},{7,5},{8,10},{9,11},{10,... | collective-permute-start | bytes 786440 | tf_op jit(solution)/shard_map/ppermute | solution.py:33
  (16 other events, 270.9 us)
where the time goes:
time: 220 us; the launch traced here: 219 us
  waiting for transfers between devices  61.4 us (28%)
  blocking collectives  48 us (22%)
  Pallas kernels  41.8 us (19%)
  starting transfers between devices  34.2 us (16%)
  other arithmetic  16.5 us (8%)
  local copies, waits for them, and re-layouts  11.1 us (5%)
  between operations  3.41 us (2%)
  matrix products  2.52 us (1%)
    all_to_all x2, blocking collectives, step(): gathered = lax.all_to_all(spread, BOTH, 0, 0, tiled=True)  48 us
    ppermute x10, waiting for transfers between devices, to_narrow(): return lax.ppermute(value, 'narrow', narrow_perm(**steps))  37.7 us
    ppermute x12, starting transfers between devices, to_wide(): return lax.ppermute(value, 'wide', wide_perm(**steps))  26.3 us
    pallas_call x2, Pallas kernels, spmm(): pl.pallas_call(spmm_kernel, grid=(2 * rows,), in_specs=[pl.BlockSpec(memo...  25.8 us
    ppermute x12, waiting for transfers between devices, to_wide(): return lax.ppermute(value, 'wide', wide_perm(**steps))  23.6 us
    pallas_call x2, Pallas kernels, pair_sum(): pl.pallas_call(pair_kernel, grid=(ZL, 2), in_specs=[pl.BlockSpec((X, 1, p...  8.41 us
    ppermute x10, starting transfers between devices, to_narrow(): return lax.ppermute(value, 'narrow', narrow_perm(**steps))  7.86 us
    convert_element_type x1, other arithmetic, step(): normed = (adjacency[0, 0].astype(jnp.float32) * row_roots[slot_rows][:, :...  4.49 us
  transfers between devices with their start and end apart: 22, of which 11 were waited for; matrix products, arithmetic and copies ran while one was open for 10% of the time, Pallas kernels for 16%

commit v1 on v0

--- a/solution.py
+++ b/solution.py
@@ -40,31 +40,27 @@
 SLOTS = 24
 ORDER, COL, SRC, START, ROWS, DEST, OWN = 0, 24, 48, 72, 89, 105, 121
 META = 128
+LANES = 128
 GRANT = 60 * 1024 * 1024
 
 
 def spmm_kernel(meta, normed, *refs):
-    pieces, (sent, kept, own), (panel, blocks, acc, sem) = refs[:Y], refs[Y : Y + 3], refs[Y + 3 :]
-    step = pl.program_id(0)
-    rows = pl.num_programs(0) // 2
+    pieces, (sent, kept, own) = refs[:Y], refs[Y : Y + 3]
+    panel, blocks, result, acc, sem_in, sem_out = refs[Y + 3 :]
+    rows = sent.shape[0]
     width = panel.shape[2]
 
-    @pl.when(step == 0)
-    def _():
-        copies = [pltpu.make_async_copy(normed, blocks, sem.at[Y * ZH])]
-        for k in range(Y):
-            for j in range(ZH):
-                target = panel.at[meta[DEST + k * ZH + j]]
-                copies.append(pltpu.make_async_copy(pieces[k].at[j], target, sem.at[k * ZH + j]))
-        for copy in copies:
-            copy.start()
-        for copy in copies:
-            copy.wait()
-        own[...] = panel[meta[OWN]]
-
-    row = meta[ROWS + step]
-    first = meta[START + row]
-    count = meta[START + row + 1] - first
+    copies = [pltpu.make_async_copy(normed, blocks, sem_in.at[Y * ZH])]
+    for k in range(Y):
+        for j in range(ZH):
+            target = panel.at[meta[DEST + k * ZH + j]]
+            copies.append(pltpu.make_async_copy(pieces[k].at[j], target, sem_in.at[k * ZH + j]))
+    for copy in copies:
+        copy.start()
+    for copy in copies:
+        copy.wait()
+    own_copy = pltpu.make_async_copy(panel.at[meta[OWN]], own, sem_out.at[2 * rows])
+    own_copy.start()
 
     def product(at):
         slot = meta[ORDER + at]
@@ -73,16 +69,20 @@
         corrupt = jnp.dot(block, panel[meta[SRC + slot]], preferred_element_type=jnp.float32)
         return clean, corrupt
 
-    def write(out):
+    def make_row(step):
+        row = meta[ROWS + step]
+        first = meta[START + row]
+        count = meta[START + row + 1] - first
+
         @pl.when(count == 0)
         def _():
-            out[...] = jnp.zeros_like(out)
+            result[step] = jnp.zeros(result.shape[1:], result.dtype)
 
         @pl.when(count == 1)
         def _():
             clean, corrupt = product(first)
-            out[0, :, :width] = clean.astype(out.dtype)
-            out[0, :, width:] = corrupt.astype(out.dtype)
+            result[step, :, :width] = clean.astype(result.dtype)
+            result[step, :, width:] = corrupt.astype(result.dtype)
 
         @pl.when(count > 1)
         def _():
@@ -95,15 +95,27 @@
                 return carry
 
             lax.fori_loop(first + 1, first + count, add_slot, 0)
-            out[0] = acc[...].astype(out.dtype)
-
-    @pl.when(step < rows)
-    def _():
-        write(sent)
-
-    @pl.when(step >= rows)
-    def _():
-        write(kept)
+            result[step] = acc[...].astype(result.dtype)
+
+    def leave(step, out, at):
+        return pltpu.make_async_copy(result.at[step], out.at[at], sem_out.at[step])
+
+    def send_row(step, carry):
+        make_row(step)
+        leave(step, sent, step).start()
+        return carry
+
+    def keep_row(step, carry):
+        make_row(step)
+        leave(step, kept, step - rows).start()
+        return carry
+
+    lax.fori_loop(0, rows, send_row, 0)
+    lax.fori_loop(rows, 2 * rows, keep_row, 0)
+    own_copy.wait()
+    for step in range(rows):
+        leave(step, sent, step).wait()
+        leave(rows + step, kept, step).wait()
 
 
 def spmm(meta, normed, pieces):
@@ -113,20 +125,17 @@
     half = jax.ShapeDtypeStruct((rows, block_len, 2 * width), jnp.bfloat16)
     return pl.pallas_call(
         spmm_kernel,
-        grid=(2 * rows,),
         in_specs=[pl.BlockSpec(memory_space=pltpu.SMEM)]
         + [pl.BlockSpec(memory_space=pl.ANY)] * (1 + len(pieces)),
-        out_specs=[
-            pl.BlockSpec((1, block_len, 2 * width), lambda i: (jnp.minimum(i, rows - 1), 0, 0)),
-            pl.BlockSpec((1, block_len, 2 * width), lambda i: (jnp.maximum(i - rows, 0), 0, 0)),
-            pl.BlockSpec((block_len, width), lambda i: (0, 0)),
-        ],
+        out_specs=[pl.BlockSpec(memory_space=pl.ANY)] * 3,
         out_shape=[half, half, jax.ShapeDtypeStruct((block_len, width), jnp.bfloat16)],
         scratch_shapes=[
             pltpu.VMEM((Y * ZH, block_len, width), jnp.bfloat16),
             pltpu.VMEM(normed.shape, normed.dtype),
+            pltpu.VMEM((2 * rows, block_len, 2 * width), jnp.bfloat16),
             pltpu.VMEM((block_len, 2 * width), jnp.float32),
             pltpu.SemaphoreType.DMA((Y * ZH + 1,)),
+            pltpu.SemaphoreType.DMA((2 * rows + 1,)),
         ],
         compiler_params=pltpu.CompilerParams(vmem_limit_bytes=GRANT),
         cost_estimate=pl.CostEstimate(
@@ -137,29 +146,53 @@
     )(meta, normed, *pieces)
 
 
-def pair_kernel(kept, arrived, *outs):
-    total = kept[...].astype(jnp.float32) + arrived[...].astype(jnp.float32)
-    for k, out in enumerate(outs):
-        out[...] = total[k].astype(out.dtype)
+def pair_kernel(kept, arrived, *refs):
+    outs, (mine, theirs, sem_mine, sem_theirs, sem_out) = refs[:X], refs[X:]
+    order = [(k, f) for k in [*range(1, X), 0] for f in range(ZL)]
+
+    def load(source, target, sem, k, f):
+        at = k * ZL + f
+        return pltpu.make_async_copy(source.at[at], target.at[at], sem.at[at])
+
+    def leave(k, f):
+        at = k * ZL + f
+        return pltpu.make_async_copy(mine.at[at], outs[k].at[f], sem_out.at[at])
+
+    for k, f in order:
+        load(kept, mine, sem_mine, k, f).start()
+        load(arrived, theirs, sem_theirs, k, f).start()
+    for k, f in order:
+        at = k * ZL + f
+        load(kept, mine, sem_mine, k, f).wait()
+        load(arrived, theirs, sem_theirs, k, f).wait()
+        total = mine[at].astype(jnp.float32) + theirs[at].astype(jnp.float32)
+        mine[at] = total.astype(mine.dtype)
+        leave(k, f).start()
+    for k, f in order:
+        leave(k, f).wait()
 
 
 def pair_sum(kept, arrived):
     rows, block_len, width = kept.shape
-    part = block_len // 2
-    shape = (X, ZL, block_len, width)
     return pl.pallas_call(
         pair_kernel,
-        grid=(ZL, 2),
-        in_specs=[pl.BlockSpec((X, 1, part, width), lambda i, j: (0, i, j, 0))] * 2,
-        out_specs=[pl.BlockSpec((1, part, width), lambda i, j: (i, j, 0))] * X,
-        out_shape=[jax.ShapeDtypeStruct(shape[1:], jnp.bfloat16)] * X,
+        in_specs=[pl.BlockSpec(memory_space=pl.ANY)] * 2,
+        out_specs=[pl.BlockSpec(memory_space=pl.ANY)] * X,
+        out_shape=[jax.ShapeDtypeStruct((ZL, block_len, width), jnp.bfloat16)] * X,
+        scratch_shapes=[
+            pltpu.VMEM(kept.shape, kept.dtype),
+            pltpu.VMEM(kept.shape, kept.dtype),
+            pltpu.SemaphoreType.DMA((rows,)),
+            pltpu.SemaphoreType.DMA((rows,)),
+            pltpu.SemaphoreType.DMA((rows,)),
+        ],
         compiler_params=pltpu.CompilerParams(vmem_limit_bytes=GRANT),
         cost_estimate=pl.CostEstimate(
             flops=rows * block_len * width,
             bytes_accessed=6 * rows * block_len * width,
             transcendentals=0,
         ),
-    )(kept.reshape(shape), arrived.reshape(shape))
+    )(kept, arrived)
 
 
 def finish_kernel(parts, width, degree, bias, own, own_corrupt, *refs):
@@ -180,7 +213,9 @@
     final = clean[...]
     hidden[...] = final.astype(hidden.dtype)
     sums = jnp.sum(final, axis=0, keepdims=True).astype(spread.dtype)
-    spread[...] = jnp.broadcast_to(sums, spread.shape)
+    for at in range(spread.shape[1]):
+        part = sums[:, at * LANES : (at + 1) * LANES][None]
+        spread[:, at : at + 1, :] = jnp.broadcast_to(part, (spread.shape[0], 1, LANES))
 
 
 def finish(devices, degree, bias, own, own_corrupt, groups):
@@ -203,20 +238,21 @@
             whole(len(groups), block_len, width),
         ]
         + ([near] * parts + [last]) * len(groups),
-        out_specs=[whole(block_len, hidden)] * 3 + [whole(devices, hidden)],
+        out_specs=[whole(block_len, hidden)] * 3 + [whole(devices, hidden // LANES, LANES)],
         out_shape=[
             jax.ShapeDtypeStruct((block_len, hidden), jnp.float32),
             jax.ShapeDtypeStruct((block_len, hidden), jnp.float32),
             jax.ShapeDtypeStruct((block_len, hidden), jnp.bfloat16),
-            jax.ShapeDtypeStruct((devices, hidden), jnp.bfloat16),
+            jax.ShapeDtypeStruct((devices, hidden // LANES, LANES), jnp.bfloat16),
         ],
         compiler_params=pltpu.CompilerParams(vmem_limit_bytes=GRANT),
     )(degree, bias, own, own_corrupt, *[value for group in groups for value in group])
 
 
 def score_kernel(nodes, gathered, disc_weight, clean, corrupt, scores, spread):
-    column_total = jnp.sum(gathered[...].astype(jnp.float32), axis=0, keepdims=True)
-    summary = jax.nn.sigmoid(column_total / nodes)
+    column_total = jnp.sum(gathered[...].astype(jnp.float32), axis=0)
+    pieces = [column_total[at : at + 1] for at in range(column_total.shape[0])]
+    summary = jax.nn.sigmoid(jnp.concatenate(pieces, axis=1) / nodes)
     lanes = (((1,), (1,)), ((), ()))
     exact = dict(precision=lax.Precision.HIGHEST, preferred_element_type=jnp.float32)
     summary = jnp.broadcast_to(summary, (8, summary.shape[1]))
@@ -245,7 +281,7 @@
     )(gathered, disc_weight, clean, corrupt)
 
 
-def step(
+def infomax(
     features,
     proj_weight,
     bias,
@@ -276,9 +312,14 @@
         part = jnp.dot(features, weight, preferred_element_type=jnp.float32)
         part = part.astype(jnp.bfloat16)
         own.append(part)
-        along_z = [part] + [to_wide(part, dz=k) for k in range(1, ZH)]
+        along_z = [part]
+        for k in range(1, ZH):
+            along_z.append(to_wide(part, dz=k))
         along_z = jnp.stack(along_z)
-        panels.append([along_z] + [to_wide(along_z, dy=k) for k in range(1, Y)])
+        panel = [along_z]
+        for k in range(1, Y):
+            panel.append(to_wide(along_z, dy=k))
+        panels.append(panel)
 
     inv_root = lax.rsqrt(degree.astype(jnp.float32))
     col_roots = lax.dynamic_index_in_dim(
@@ -343,7 +384,9 @@
         own_corrupt.append(own_part)
         arrived = to_narrow(sent, flip_core=1)
         halves = pair_sum(kept, arrived)
-        got = [halves[0]] + [to_narrow(halves[k], dx=k) for k in range(1, X)]
+        got = [halves[0]]
+        for k in range(1, X):
+            got.append(to_narrow(halves[k], dx=k))
         far = sum(value[1].astype(jnp.float32) for value in got).astype(jnp.bfloat16)
         last = to_narrow(far, flip_z=1)
         groups.append(got + [last])
@@ -361,7 +404,7 @@
         jnp.stack(own_corrupt),
         groups,
     )
-    gathered = lax.all_to_all(spread, BOTH, 0, 0, tiled=True)
+    gathered = lax.all_to_all(spread, BOTH, 0, 0)
     scores, spread = score(nodes, devices, gathered, disc_weight, clean_h, corrupt_h)
     gathered = lax.all_to_all(spread, BOTH, 0, 0, tiled=True)
     loss = jnp.sum(gathered[:, 0]) / (2 * nodes)
@@ -382,7 +425,7 @@
         P(),
     )
     return jax.shard_map(
-        step,
+        infomax,
         mesh=mesh,
         in_specs=placed,
         out_specs=(P(("wide", "narrow"), None), P(None, ("wide", "narrow")), P()),

time: 220 us -> 213 us (0.968)
  Pallas kernels: 41.8 us -> 35.2 us
  waiting for transfers between devices: 61.4 us -> 64.3 us
    pallas_call x4, Pallas kernels: 34.2 us -> 27.4 us  [the longest x2 20.7 us: spmm(): pl.pallas_call(spmm_kernel, in_specs=[pl.BlockSpec(memory_space=pltpu.SME...]
    ppermute x12, waiting for transfers between devices: 23.6 us -> 26.4 us  [to_wide(): return lax.ppermute(value, 'wide', wide_perm(**steps))]
  transfers between devices with their start and end apart: 22 -> 22, of which waited for: 11 -> 14; matrix products, arithmetic and copies ran while one was open for 10% -> 10% of each run, Pallas kernels for 16% -> 13%
where the time goes in v1:
time: 213 us; the launch traced here: 212 us
  waiting for transfers between devices  64.3 us (30%)
  blocking collectives  49.8 us (23%)
  Pallas kernels  35.2 us (17%)
  starting transfers between devices  33.1 us (16%)
  other arithmetic  14.5 us (7%)
  local copies, waits for them, and re-layouts  9.54 us (4%)
  between operations  3.43 us (2%)
  matrix products  2.52 us (1%)
    ppermute x10, waiting for transfers between devices, to_narrow(): return lax.ppermute(value, 'narrow', narrow_perm(**steps))  37.9 us
    all_to_all x1, blocking collectives, infomax(): gathered = lax.all_to_all(spread, BOTH, 0, 0)  30.7 us
    ppermute x12, waiting for transfers between devices, to_wide(): return lax.ppermute(value, 'wide', wide_perm(**steps))  26.4 us
    ppermute x12, starting transfers between devices, to_wide(): return lax.ppermute(value, 'wide', wide_perm(**steps))  26.3 us
    pallas_call x2, Pallas kernels, spmm(): pl.pallas_call(spmm_kernel, in_specs=[pl.BlockSpec(memory_space=pltpu.SME...  20.7 us
    all_to_all x1, blocking collectives, infomax(): gathered = lax.all_to_all(spread, BOTH, 0, 0, tiled=True)  19.1 us
    ppermute x10, starting transfers between devices, to_narrow(): return lax.ppermute(value, 'narrow', narrow_perm(**steps))  6.8 us
    pallas_call x2, Pallas kernels, pair_sum(): pl.pallas_call(pair_kernel, in_specs=[pl.BlockSpec(memory_space=pl.ANY)]...  6.69 us
  transfers between devices with their start and end apart: 22, of which 14 were waited for; matrix products, arithmetic and copies ran while one was open for 10% of the time, Pallas kernels for 13%

profile of v1, /device:TPU:1, one launch (start us, length us, event | category | flops | bytes accessed | tf_op | source)
XLA Modules:
  0.0 212.4 jit_solution(9342551938754442015)
XLA Ops:
  2.9 3.9 %collective-permute-start.6 = (bf16[256,256]{1,0:T(8,128)(2,1)S(1)}, bf16[256,256]{1,0:T(8,128)(2,1)S(1)}, u32[]{:S(2)}, u32[]{:S(2)}) collective-permute-start(bf16[256,256]{1,0:T(8,128)(2,1)S(1)} %convolution_convert_fusion), channel_id=1, source_target_pairs={{0,16},{16,32},{32,48},{48,0},{64,80},{80,96},{96,112},{112,64},{1... | collective-permute-start | bytes 393224 | tf_op jit(solution)/shard_map/ppermute | solution.py:37
  6.8 5.1 %collective-permute-start.7 = (bf16[256,256]{1,0:T(8,128)(2,1)S(1)}, bf16[256,256]{1,0:T(8,128)(2,1)S(1)}, u32[]{:S(2)}, u32[]{:S(2)}) collective-permute-start(bf16[256,256]{1,0:T(8,128)(2,1)S(1)} %convolution_convert_fusion), channel_id=1, source_target_pairs={{0,32},{16,48},{32,0},{48,16},{64,96},{80,112},{96,64},{112,80},{1... | collective-permute-start | bytes 393224 | tf_op jit(solution)/shard_map/ppermute | solution.py:37
  11.9 2.4 %collective-permute-start.8 = (bf16[256,256]{1,0:T(8,128)(2,1)S(1)}, bf16[256,256]{1,0:T(8,128)(2,1)S(1)}, u32[]{:S(2)}, u32[]{:S(2)}) collective-permute-start(bf16[256,256]{1,0:T(8,128)(2,1)S(1)} %convolution_convert_fusion), channel_id=1, source_target_pairs={{0,48},{16,0},{32,16},{48,32},{64,112},{80,64},{96,80},{112,96},{1... | collective-permute-start | bytes 393224 | tf_op jit(solution)/shard_map/ppermute | solution.py:37
  22.6 4.5 %fusion.1.normed = bf16[24,256,256]{2,1,0:T(8,128)(2,1)} fusion(s32[1,1,24,256,256]{4,3,2,1,0:T(8,128)} %param.14, f32[24,256]{1,0:T(8,128)S(1)} %gather_fusion.1, f32[24,256]{1,0:T(8,128)S(1)} %gather_fusion), kind=kLoop, calls=%fused_computation.4 | loop fusion | flops 6291456 | bytes 9486336 | tf_op jit(solution)/shard_map/convert_element_type | solution.py:337
  27.1 3.4 %collective-permute-done.8 = bf16[256,256]{1,0:T(8,128)(2,1)S(1)} collective-permute-done((bf16[256,256]{1,0:T(8,128)(2,1)S(1)}, bf16[256,256]{1,0:T(8,128)(2,1)S(1)}, u32[]{:S(2)}, u32[]{:S(2)}) %collective-permute-start.8) | collective-permute-done | bytes 131104 | tf_op jit(solution)/shard_map/ppermute | solution.py:37
  30.5 3.0 %collective-permute-start.10 = (bf16[4,256,256]{2,1,0:T(8,128)(2,1)S(1)}, bf16[4,256,256]{2,1,0:T(8,128)(2,1)S(1)}, u32[]{:S(2)}, u32[]{:S(2)}) collective-permute-start(bf16[4,256,256]{2,1,0:T(8,128)(2,1)S(1)} %pad_maximum_fusion.1.refs_0_), channel_id=1, source_target_pairs={{0,128},{16,144},{32,160},{48,176},{64,192},{80,208},{96,224},{112... | collective-permute-start | bytes 1572872 | tf_op jit(solution)/shard_map/ppermute | solution.py:37
  35.3 3.4 %collective-permute-start.2 = (bf16[256,256]{1,0:T(8,128)(2,1)S(1)}, bf16[256,256]{1,0:T(8,128)(2,1)S(1)}, u32[]{:S(2)}, u32[]{:S(2)}) collective-permute-start(bf16[256,256]{1,0:T(8,128)(2,1)S(1)} %convolution_convert_fusion.1), channel_id=1, source_target_pairs={{0,48},{16,0},{32,16},{48,32},{64,112},{80,64},{96,80},{112,96},{1... | collective-permute-start | bytes 393224 | tf_op jit(solution)/shard_map/ppermute | solution.py:37
  39.2 3.8 %collective-permute-done.2 = bf16[256,256]{1,0:T(8,128)(2,1)S(1)} collective-permute-done((bf16[256,256]{1,0:T(8,128)(2,1)S(1)}, bf16[256,256]{1,0:T(8,128)(2,1)S(1)}, u32[]{:S(2)}, u32[]{:S(2)}) %collective-permute-start.2) | collective-permute-done | bytes 131104 | tf_op jit(solution)/shard_map/ppermute | solution.py:37
  43.7 2.5 %collective-permute-start.4 = (bf16[4,256,256]{2,1,0:T(8,128)(2,1)S(1)}, bf16[4,256,256]{2,1,0:T(8,128)(2,1)}, u32[]{:S(2)}, u32[]{:S(2)}) collective-permute-start(bf16[4,256,256]{2,1,0:T(8,128)(2,1)S(1)} %pad_maximum_fusion.refs_0_), channel_id=1, source_target_pairs={{0,128},{16,144},{32,160},{48,176},{64,192},{80,208},{96,224},{112... | collective-permute-start | bytes 1572872 | tf_op jit(solution)/shard_map/ppermute | solution.py:37
  49.1 7.7 %collective-permute-done.11.refs_3_ = bf16[4,256,256]{2,1,0:T(8,128)(2,1)S(1)} collective-permute-done((bf16[4,256,256]{2,1,0:T(8,128)(2,1)S(1)}, bf16[4,256,256]{2,1,0:T(8,128)(2,1)S(1)}, u32[]{:S(2)}, u32[]{:S(2)}) %collective-permute-start.11) | collective-permute-done | bytes 524320 | tf_op jit(solution)/shard_map/ppermute | solution.py:37
  57.6 10.3 %shard_map.122 = (bf16[8,256,512]{2,1,0:T(8,128)(2,1)}, bf16[8,256,512]{2,1,0:T(8,128)(2,1)}, bf16[256,256]{1,0:T(8,128)(2,1)}) custom-call(s32[128]{0:T(128)} %concatenate.7.meta, bf16[24,256,256]{2,1,0:T(8,128)(2,1)} %fusion.1.normed, bf16[4,256,256]{2,1,0:T(8,128)(2,1)} %copy-done.8, bf16[4,256,256]{2,1,0:T(8,128)(2,1)} %collective-permute-done.9.refs_1_, ...), custom_call_target="tpu_custom_call" | custom-call | flops 1610612736 | bytes 10485760 | tf_op jit(solution)/shard_map/pallas_call | solution.py:126
  69.4 9.6 %collective-permute-done.4.refs_2_ = bf16[4,256,256]{2,1,0:T(8,128)(2,1)} collective-permute-done((bf16[4,256,256]{2,1,0:T(8,128)(2,1)S(1)}, bf16[4,256,256]{2,1,0:T(8,128)(2,1)}, u32[]{:S(2)}, u32[]{:S(2)}) %collective-permute-start.4) | collective-permute-done | bytes 524320 | tf_op jit(solution)/shard_map/ppermute | solution.py:37
  79.4 10.3 %shard_map.121 = (bf16[8,256,512]{2,1,0:T(8,128)(2,1)}, bf16[8,256,512]{2,1,0:T(8,128)(2,1)}, bf16[256,256]{1,0:T(8,128)(2,1)}) custom-call(s32[128]{0:T(128)} %concatenate.7.meta, bf16[24,256,256]{2,1,0:T(8,128)(2,1)} %fusion.1.normed, bf16[4,256,256]{2,1,0:T(8,128)(2,1)} %copy-done.9, bf16[4,256,256]{2,1,0:T(8,128)(2,1)} %collective-permute-done.3.refs_1_, ...), custom_call_target="tpu_custom_call" | custom-call | flops 1610612736 | bytes 10485760 | tf_op jit(solution)/shard_map/pallas_call | solution.py:126
  91.1 3.3 %shard_map.124 = (bf16[2,256,512]{2,1,0:T(8,128)(2,1)}, bf16[2,256,512]{2,1,0:T(8,128)(2,1)}, bf16[2,256,512]{2,1,0:T(8,128)(2,1)}, bf16[2,256,512]{2,1,0:T(8,128)(2,1)}) custom-call(bf16[8,256,512]{2,1,0:T(8,128)(2,1)} %get-tuple-element.31.kept, bf16[8,256,512]{2,1,0:T(8,128)(2,1)} %copy-done.1), custom_call_target="tpu_custom_call" | custom-call | flops 1048576 | bytes 6291456 | tf_op jit(solution)/shard_map/pallas_call | solution.py:177
  94.6 2.3 %collective-permute-start.19 = (bf16[2,256,512]{2,1,0:T(8,128)(2,1)}, bf16[2,256,512]{2,1,0:T(8,128)(2,1)S(1)}, u32[]{:S(2)}, u32[]{:S(2)}) collective-permute-start(bf16[2,256,512]{2,1,0:T(8,128)(2,1)} %get-tuple-element.35), channel_id=1, source_target_pairs={{0,8},{1,9},{2,10},{3,11},{4,12},{5,13},{6,14},{7,15},{8,0},{9,1},... | collective-permute-start | bytes 1572872 | tf_op jit(solution)/shard_map/ppermute | solution.py:33
  97.3 3.3 %shard_map.123 = (bf16[2,256,512]{2,1,0:T(8,128)(2,1)}, bf16[2,256,512]{2,1,0:T(8,128)(2,1)}, bf16[2,256,512]{2,1,0:T(8,128)(2,1)}, bf16[2,256,512]{2,1,0:T(8,128)(2,1)}) custom-call(bf16[8,256,512]{2,1,0:T(8,128)(2,1)} %get-tuple-element.25.kept, bf16[8,256,512]{2,1,0:T(8,128)(2,1)} %collective-permute-done.12.arrived), custom_call_target="tpu_custom_call" | custom-call | flops 1048576 | bytes 6291456 | tf_op jit(solution)/shard_map/pallas_call | solution.py:177
  103.2 5.8 %collective-permute-done.18.refs_6_ = bf16[2,256,512]{2,1,0:T(8,128)(2,1)S(1)} collective-permute-done((bf16[2,256,512]{2,1,0:T(8,128)(2,1)}, bf16[2,256,512]{2,1,0:T(8,128)(2,1)S(1)}, u32[]{:S(2)}, u32[]{:S(2)}) %collective-permute-start.18) | collective-permute-done | bytes 524320 | tf_op jit(solution)/shard_map/ppermute | solution.py:33
  111.1 9.3 %collective-permute-done.19.refs_7_ = bf16[2,256,512]{2,1,0:T(8,128)(2,1)S(1)} collective-permute-done((bf16[2,256,512]{2,1,0:T(8,128)(2,1)}, bf16[2,256,512]{2,1,0:T(8,128)(2,1)S(1)}, u32[]{:S(2)}, u32[]{:S(2)}) %collective-permute-start.19) | collective-permute-done | bytes 524320 | tf_op jit(solution)/shard_map/ppermute | solution.py:33
  122.2 9.2 %collective-permute-done.13.refs_1_ = bf16[2,256,512]{2,1,0:T(8,128)(2,1)S(1)} collective-permute-done((bf16[2,256,512]{2,1,0:T(8,128)(2,1)}, bf16[2,256,512]{2,1,0:T(8,128)(2,1)S(1)}, u32[]{:S(2)}, u32[]{:S(2)}) %collective-permute-start.13) | collective-permute-done | bytes 524320 | tf_op jit(solution)/shard_map/ppermute | solution.py:33
  131.5 11.4 %collective-permute-done.14.refs_2_ = bf16[2,256,512]{2,1,0:T(8,128)(2,1)S(1)} collective-permute-done((bf16[2,256,512]{2,1,0:T(8,128)(2,1)}, bf16[2,256,512]{2,1,0:T(8,128)(2,1)S(1)}, u32[]{:S(2)}, u32[]{:S(2)}) %collective-permute-start.14) | collective-permute-done | bytes 524320 | tf_op jit(solution)/shard_map/ppermute | solution.py:33
  152.3 3.5 %shard_map.125 = (f32[256,512]{1,0:T(8,128)}, f32[256,512]{1,0:T(8,128)}, bf16[256,512]{1,0:T(8,128)(2,1)}, bf16[256,4,128]{2,1,0:T(4,128)(2,1)}) custom-call(f32[256,1]{1,0:T(8,128)} %copy.27.degree, f32[1,512]{1,0:T(1,128)} %bitcast.61, bf16[256,512]{1,0:T(8,128)(2,1)} %pad_maximum_fusion.2.own, bf16[2,256,256]{2,1,0:T(8,128)(2,1)} %pad_maximum_fusion.3.own_corrupt, ...), custom_call_target="tpu_custom_call" | custom-call | tf_op jit(solution)/shard_map/pallas_call | solution.py:231
  155.8 30.7 %all_to_all.17.gathered = bf16[256,4,128]{2,1,0:T(4,128)(2,1)} all-to-all(bf16[256,4,128]{2,1,0:T(4,128)(2,1)} %get-tuple-element.38), channel_id=1, replica_groups=mesh['wide'=16,'narrow'=16] {'wide','narrow'}, dimensions={0} | all-to-all | bytes 524288 | tf_op jit(solution)/shard_map/all_to_all | solution.py:407
  186.5 4.4 %shard_map.126 = (f32[2,256]{1,0:T(2,128)}, f32[256,128]{1,0:T(8,128)}) custom-call(bf16[256,4,128]{2,1,0:T(4,128)(2,1)} %all_to_all.17.gathered, f32[512,512]{1,0:T(8,128)} %disc_weight.1, f32[256,512]{1,0:T(8,128)} %get-tuple-element.39.clean, f32[256,512]{1,0:T(8,128)} %get-tuple-element.40.corrupt), custom_call_target="tpu_custom_call" | custom-call | tf_op jit(solution)/shard_map/pallas_call | solution.py:274
  190.9 19.1 %all_to_all.18 = f32[256,1,128]{2,1,0:T(1,128)S(1)} all-to-all(f32[256,1,128]{2,1,0:T(1,128)} %bitcast.52), channel_id=1, replica_groups=mesh['wide'=16,'narrow'=16] {'wide','narrow'}, dimensions={0} | all-to-all | bytes 262144 | tf_op jit(solution)/shard_map/all_to_all | solution.py:409
  (105 shorter events, 36.6 us)
Async XLA Ops:
  2.9 24.1 %collective-permute-start.6 = (bf16[256,256]{1,0:T(8,128)(2,1)S(1)}, bf16[256,256]{1,0:T(8,128)(2,1)S(1)}, u32[]{:S(2)}, u32[]{:S(2)}) collective-permute-start(bf16[256,256]{1,0:T(8,128)(2,1)S(1)} %convolution_convert_fusion), channel_id=1, source_target_pairs={{0,16},{16,32},{32,48},{48,0},{64,80},{80,96},{96,112},{112,64},{1... | collective-permute-start | bytes 393224 | tf_op jit(solution)/shard_map/ppermute | solution.py:37
  6.8 20.3 %collective-permute-start.7 = (bf16[256,256]{1,0:T(8,128)(2,1)S(1)}, bf16[256,256]{1,0:T(8,128)(2,1)S(1)}, u32[]{:S(2)}, u32[]{:S(2)}) collective-permute-start(bf16[256,256]{1,0:T(8,128)(2,1)S(1)} %convolution_convert_fusion), channel_id=1, source_target_pairs={{0,32},{16,48},{32,0},{48,16},{64,96},{80,112},{96,64},{112,80},{1... | collective-permute-start | bytes 393224 | tf_op jit(solution)/shard_map/ppermute | solution.py:37
  11.9 18.6 %collective-permute-start.8 = (bf16[256,256]{1,0:T(8,128)(2,1)S(1)}, bf16[256,256]{1,0:T(8,128)(2,1)S(1)}, u32[]{:S(2)}, u32[]{:S(2)}) collective-permute-start(bf16[256,256]{1,0:T(8,128)(2,1)S(1)} %convolution_convert_fusion), channel_id=1, source_target_pairs={{0,48},{16,0},{32,16},{48,32},{64,112},{80,64},{96,80},{112,96},{1... | collective-permute-start | bytes 393224 | tf_op jit(solution)/shard_map/ppermute | solution.py:37
  15.6 52.4 %copy-start.11 = (bf16[256,256]{1,0:T(8,128)(2,1)}, bf16[256,256]{1,0:T(8,128)(2,1)S(1)}, u32[]{:S(2)}) copy-start(bf16[256,256]{1,0:T(8,128)(2,1)S(1)} %convolution_convert_fusion.1) | copy-start | bytes 393220
  15.6 19.7 %collective-permute-start = (bf16[256,256]{1,0:T(8,128)(2,1)S(1)}, bf16[256,256]{1,0:T(8,128)(2,1)S(1)}, u32[]{:S(2)}, u32[]{:S(2)}) collective-permute-start(bf16[256,256]{1,0:T(8,128)(2,1)S(1)} %convolution_convert_fusion.1), channel_id=1, source_target_pairs={{0,16},{16,32},{32,48},{48,0},{64,80},{80,96},{96,112},{112,64},{1... | collective-permute-start | bytes 393224 | tf_op jit(solution)/shard_map/ppermute | solution.py:37
  15.7 23.5 %collective-permute-start.1 = (bf16[256,256]{1,0:T(8,128)(2,1)S(1)}, bf16[256,256]{1,0:T(8,128)(2,1)S(1)}, u32[]{:S(2)}, u32[]{:S(2)}) collective-permute-start(bf16[256,256]{1,0:T(8,128)(2,1)S(1)} %convolution_convert_fusion.1), channel_id=1, source_target_pairs={{0,32},{16,48},{32,0},{48,16},{64,96},{80,112},{96,64},{112,80},{1... | collective-permute-start | bytes 393224 | tf_op jit(solution)/shard_map/ppermute | solution.py:37
  30.5 15.6 %collective-permute-start.10 = (bf16[4,256,256]{2,1,0:T(8,128)(2,1)S(1)}, bf16[4,256,256]{2,1,0:T(8,128)(2,1)S(1)}, u32[]{:S(2)}, u32[]{:S(2)}) collective-permute-start(bf16[4,256,256]{2,1,0:T(8,128)(2,1)S(1)} %pad_maximum_fusion.1.refs_0_), channel_id=1, source_target_pairs={{0,128},{16,144},{32,160},{48,176},{64,192},{80,208},{96,224},{112... | collective-permute-start | bytes 1572872 | tf_op jit(solution)/shard_map/ppermute | solution.py:37
  33.5 23.3 %collective-permute-start.11 = (bf16[4,256,256]{2,1,0:T(8,128)(2,1)S(1)}, bf16[4,256,256]{2,1,0:T(8,128)(2,1)S(1)}, u32[]{:S(2)}, u32[]{:S(2)}) collective-permute-start(bf16[4,256,256]{2,1,0:T(8,128)(2,1)S(1)} %pad_maximum_fusion.1.refs_0_), channel_id=1, source_target_pairs={{0,192},{16,208},{32,224},{48,240},{64,0},{80,16},{96,32},{112,48}... | collective-permute-start | bytes 1572872 | tf_op jit(solution)/shard_map/ppermute | solution.py:37
  34.3 23.0 %collective-permute-start.9 = (bf16[4,256,256]{2,1,0:T(8,128)(2,1)S(1)}, bf16[4,256,256]{2,1,0:T(8,128)(2,1)}, u32[]{:S(2)}, u32[]{:S(2)}) collective-permute-start(bf16[4,256,256]{2,1,0:T(8,128)(2,1)S(1)} %pad_maximum_fusion.1.refs_0_), channel_id=1, source_target_pairs={{0,64},{16,80},{32,96},{48,112},{64,128},{80,144},{96,160},{112,17... | collective-permute-start | bytes 1572872 | tf_op jit(solution)/shard_map/ppermute | solution.py:37
  35.3 7.6 %collective-permute-start.2 = (bf16[256,256]{1,0:T(8,128)(2,1)S(1)}, bf16[256,256]{1,0:T(8,128)(2,1)S(1)}, u32[]{:S(2)}, u32[]{:S(2)}) collective-permute-start(bf16[256,256]{1,0:T(8,128)(2,1)S(1)} %convolution_convert_fusion.1), channel_id=1, source_target_pairs={{0,48},{16,0},{32,16},{48,32},{64,112},{80,64},{96,80},{112,96},{1... | collective-permute-start | bytes 393224 | tf_op jit(solution)/shard_map/ppermute | solution.py:37
  43.0 26.4 %collective-permute-start.3 = (bf16[4,256,256]{2,1,0:T(8,128)(2,1)S(1)}, bf16[4,256,256]{2,1,0:T(8,128)(2,1)}, u32[]{:S(2)}, u32[]{:S(2)}) collective-permute-start(bf16[4,256,256]{2,1,0:T(8,128)(2,1)S(1)} %pad_maximum_fusion.refs_0_), channel_id=1, source_target_pairs={{0,64},{16,80},{32,96},{48,112},{64,128},{80,144},{96,160},{112,17... | collective-permute-start | bytes 1572872 | tf_op jit(solution)/shard_map/ppermute | solution.py:37
  43.7 35.3 %collective-permute-start.4 = (bf16[4,256,256]{2,1,0:T(8,128)(2,1)S(1)}, bf16[4,256,256]{2,1,0:T(8,128)(2,1)}, u32[]{:S(2)}, u32[]{:S(2)}) collective-permute-start(bf16[4,256,256]{2,1,0:T(8,128)(2,1)S(1)} %pad_maximum_fusion.refs_0_), channel_id=1, source_target_pairs={{0,128},{16,144},{32,160},{48,176},{64,192},{80,208},{96,224},{112... | collective-permute-start | bytes 1572872 | tf_op jit(solution)/shard_map/ppermute | solution.py:37
  46.2 33.2 %collective-permute-start.5 = (bf16[4,256,256]{2,1,0:T(8,128)(2,1)S(1)}, bf16[4,256,256]{2,1,0:T(8,128)(2,1)}, u32[]{:S(2)}, u32[]{:S(2)}) collective-permute-start(bf16[4,256,256]{2,1,0:T(8,128)(2,1)S(1)} %pad_maximum_fusion.refs_0_), channel_id=1, source_target_pairs={{0,192},{16,208},{32,224},{48,240},{64,0},{80,16},{96,32},{112,48}... | collective-permute-start | bytes 1572872 | tf_op jit(solution)/shard_map/ppermute | solution.py:37
  68.0 21.8 %collective-permute-start.17 = (bf16[8,256,512]{2,1,0:T(8,128)(2,1)}, bf16[8,256,512]{2,1,0:T(8,128)(2,1)S(1)}, u32[]{:S(2)}, u32[]{:S(2)}) collective-permute-start(bf16[8,256,512]{2,1,0:T(8,128)(2,1)} %get-tuple-element.32), channel_id=1, source_target_pairs={{0,1},{1,0},{2,3},{3,2},{4,5},{5,4},{6,7},{7,6},{8,9},{9,8},{10,11... | collective-permute-start | bytes 6291464 | tf_op jit(solution)/shard_map/ppermute | solution.py:33
  89.7 7.5 %collective-permute-start.12 = (bf16[8,256,512]{2,1,0:T(8,128)(2,1)}, bf16[8,256,512]{2,1,0:T(8,128)(2,1)}, u32[]{:S(2)}, u32[]{:S(2)}) collective-permute-start(bf16[8,256,512]{2,1,0:T(8,128)(2,1)} %get-tuple-element.26), channel_id=1, source_target_pairs={{0,1},{1,0},{2,3},{3,2},{4,5},{5,4},{6,7},{7,6},{8,9},{9,8},{10,11... | collective-permute-start | bytes 6291464 | tf_op jit(solution)/shard_map/ppermute | solution.py:33
  94.5 14.5 %collective-permute-start.18 = (bf16[2,256,512]{2,1,0:T(8,128)(2,1)}, bf16[2,256,512]{2,1,0:T(8,128)(2,1)S(1)}, u32[]{:S(2)}, u32[]{:S(2)}) collective-permute-start(bf16[2,256,512]{2,1,0:T(8,128)(2,1)} %get-tuple-element.34), channel_id=1, source_target_pairs={{0,4},{1,5},{2,6},{3,7},{4,8},{5,9},{6,10},{7,11},{8,12},{9,13},{1... | collective-permute-start | bytes 1572872 | tf_op jit(solution)/shard_map/ppermute | solution.py:33
  94.6 25.8 %collective-permute-start.19 = (bf16[2,256,512]{2,1,0:T(8,128)(2,1)}, bf16[2,256,512]{2,1,0:T(8,128)(2,1)S(1)}, u32[]{:S(2)}, u32[]{:S(2)}) collective-permute-start(bf16[2,256,512]{2,1,0:T(8,128)(2,1)} %get-tuple-element.35), channel_id=1, source_target_pairs={{0,8},{1,9},{2,10},{3,11},{4,12},{5,13},{6,14},{7,15},{8,0},{9,1},... | collective-permute-start | bytes 1572872 | tf_op jit(solution)/shard_map/ppermute | solution.py:33
  96.9 23.7 %collective-permute-start.20 = (bf16[2,256,512]{2,1,0:T(8,128)(2,1)}, bf16[2,256,512]{2,1,0:T(8,128)(2,1)S(1)}, u32[]{:S(2)}, u32[]{:S(2)}) collective-permute-start(bf16[2,256,512]{2,1,0:T(8,128)(2,1)} %get-tuple-element.36), channel_id=1, source_target_pairs={{0,12},{1,13},{2,14},{3,15},{4,0},{5,1},{6,2},{7,3},{8,4},{9,5},{1... | collective-permute-start | bytes 1572872 | tf_op jit(solution)/shard_map/ppermute | solution.py:33
  100.6 30.9 %collective-permute-start.13 = (bf16[2,256,512]{2,1,0:T(8,128)(2,1)}, bf16[2,256,512]{2,1,0:T(8,128)(2,1)S(1)}, u32[]{:S(2)}, u32[]{:S(2)}) collective-permute-start(bf16[2,256,512]{2,1,0:T(8,128)(2,1)} %get-tuple-element.28), channel_id=1, source_target_pairs={{0,4},{1,5},{2,6},{3,7},{4,8},{5,9},{6,10},{7,11},{8,12},{9,13},{1... | collective-permute-start | bytes 1572872 | tf_op jit(solution)/shard_map/ppermute | solution.py:33
  101.8 41.1 %collective-permute-start.14 = (bf16[2,256,512]{2,1,0:T(8,128)(2,1)}, bf16[2,256,512]{2,1,0:T(8,128)(2,1)S(1)}, u32[]{:S(2)}, u32[]{:S(2)}) collective-permute-start(bf16[2,256,512]{2,1,0:T(8,128)(2,1)} %get-tuple-element.29), channel_id=1, source_target_pairs={{0,8},{1,9},{2,10},{3,11},{4,12},{5,13},{6,14},{7,15},{8,0},{9,1},... | collective-permute-start | bytes 1572872 | tf_op jit(solution)/shard_map/ppermute | solution.py:33
  109.0 42.6 %copy-start.3 = (bf16[2,256,512]{2,1,0:T(8,128)(2,1)}, bf16[2,256,512]{2,1,0:T(8,128)(2,1)S(1)}, u32[]{:S(2)}) copy-start(bf16[2,256,512]{2,1,0:T(8,128)(2,1)S(1)} %collective-permute-done.18.refs_6_) | copy-start | bytes 1572868
  109.0 34.2 %collective-permute-start.15 = (bf16[2,256,512]{2,1,0:T(8,128)(2,1)}, bf16[2,256,512]{2,1,0:T(8,128)(2,1)}, u32[]{:S(2)}, u32[]{:S(2)}) collective-permute-start(bf16[2,256,512]{2,1,0:T(8,128)(2,1)} %get-tuple-element.30), channel_id=1, source_target_pairs={{0,12},{1,13},{2,14},{3,15},{4,0},{5,1},{6,2},{7,3},{8,4},{9,5},{1... | collective-permute-start | bytes 1572872 | tf_op jit(solution)/shard_map/ppermute | solution.py:33
  121.5 28.5 %collective-permute-start.21 = (bf16[256,512]{1,0:T(8,128)(2,1)}, bf16[256,512]{1,0:T(8,128)(2,1)S(1)}, u32[]{:S(2)}, u32[]{:S(2)}) collective-permute-start(bf16[256,512]{1,0:T(8,128)(2,1)} %fusion.5), channel_id=1, source_target_pairs={{0,2},{1,3},{2,0},{3,1},{4,6},{5,7},{6,4},{7,5},{8,10},{9,11},{10,... | collective-permute-start | bytes 786440 | tf_op jit(solution)/shard_map/ppermute | solution.py:33
  145.1 6.5 %collective-permute-start.16 = (bf16[256,512]{1,0:T(8,128)(2,1)}, bf16[256,512]{1,0:T(8,128)(2,1)S(1)}, u32[]{:S(2)}, u32[]{:S(2)}) collective-permute-start(bf16[256,512]{1,0:T(8,128)(2,1)} %fusion.4), channel_id=1, source_target_pairs={{0,2},{1,3},{2,0},{3,1},{4,6},{5,7},{6,4},{7,5},{8,10},{9,11},{10,... | collective-permute-start | bytes 786440 | tf_op jit(solution)/shard_map/ppermute | solution.py:33
  (16 other events, 265.5 us)

commit v2 on v1

v2 whole, which is shorter than its diff:
```python
import functools

import jax
import jax.numpy as jnp
from jax import lax
from jax.experimental import pallas as pl
from jax.experimental.pallas import tpu as pltpu
from jax.sharding import PartitionSpec as P


X, ZL, CORES = 4, 2, 2
Y, ZH = 4, 4
BOTH = ("wide", "narrow")


def narrow_perm(dx=0, flip_z=0, flip_core=0):
    pairs = []
    for x in range(X):
        for zl in range(ZL):
            for core in range(CORES):
                target = (((x + dx) % X) * ZL + (zl ^ flip_z)) * CORES + (core ^ flip_core)
                pairs.append(((x * ZL + zl) * CORES + core, target))
    return pairs


def wide_perm(dy=0, dz=0):
    return [
        (y * ZH + zh, ((y + dy) % Y) * ZH + (zh + dz) % ZH) for y in range(Y) for zh in range(ZH)
    ]


def to_narrow(value, **steps):
    return lax.ppermute(value, "narrow", narrow_perm(**steps))


def to_wide(value, **steps):
    return lax.ppermute(value, "wide", wide_perm(**steps))


SLOTS = 24
ORDER, COL, SRC, START, ROWS, DEST, OWN = 0, 48, 96, 144, 161, 169, 185
META = 256
LANES = 128
MIB = 1024 * 1024


def products_kernel(split, meta, normed, other_normed, *refs):
    pieces, refs = refs[: 2 * Y], refs[2 * Y :]
    sides, refs = refs[: ZL * split], refs[ZL * split :]
    outs, own = refs[:X], refs[X]
    panel, blocks, result, acc, sem_panel, sem_block, sem_out = refs[X + 1 :]
    rows = X * ZL
    width = panel.shape[2]

    copies = []
    for k in range(Y):
        for j in range(ZH):
            at = meta[DEST + k * ZH + j]
            for core in range(CORES):
                copies.append(
                    pltpu.make_async_copy(
                        pieces[core * Y + k].at[j],
                        panel.at[core * Y * ZH + at],
                        sem_panel.at[(k * ZH + j) * CORES + core],
                    )
                )
    for copy in copies:
        copy.start()

    def span(step):
        row = meta[ROWS + step]
        return meta[START + row], meta[START + row + 1]

    def fetch_row(step, carry):
        def fetch(at, carry):
            slot = meta[ORDER + at]

            @pl.when(slot < SLOTS)
            def _():
                pltpu.make_async_copy(normed.at[slot], blocks.at[slot], sem_block.at[slot]).start()

            @pl.when(slot >= SLOTS)
            def _():
                pltpu.make_async_copy(
                    other_normed.at[slot - SLOTS], blocks.at[slot], sem_block.at[slot]
                ).start()

            return carry

        return lax.fori_loop(*span(step), fetch, carry)

    lax.fori_loop(0, rows, fetch_row, 0)
    for copy in copies:
        copy.wait()
    own_copy = pltpu.make_async_copy(panel.at[meta[OWN]], own, sem_out.at[2 * rows])
    own_copy.start()

    def product(at):
        slot = meta[ORDER + at]
        pltpu.make_async_copy(normed.at[0], blocks.at[slot], sem_block.at[slot]).wait()
        block = blocks[slot]
        clean = jnp.dot(block, panel[meta[COL + slot]], preferred_element_type=jnp.float32)
        corrupt = jnp.dot(block, panel[meta[SRC + slot]], preferred_element_type=jnp.float32)
        return clean, corrupt

    def make_row(step):
        first, end = span(step)
        count = end - first

        @pl.when(count == 0)
        def _():
            result[step] = jnp.zeros(result.shape[1:], result.dtype)

        @pl.when(count == 1)
        def _():
            clean, corrupt = product(first)
            result[step, :, :width] = clean.astype(result.dtype)
            result[step, :, width:] = corrupt.astype(result.dtype)

        @pl.when(count > 1)
        def _():
            acc[:, :width], acc[:, width:] = product(first)

            def add_slot(at, carry):
                clean, corrupt = product(at)
                acc[:, :width] += clean
                acc[:, width:] += corrupt
                return carry

            lax.fori_loop(first + 1, end, add_slot, 0)
            result[step] = acc[...].astype(result.dtype)

    def leave(k, f):
        step = k * ZL + f
        row = result.at[step]
        if not split:
            return [pltpu.make_async_copy(row, outs[k].at[f], sem_out.at[step])]
        clean, corrupt = row.at[:, pl.ds(0, width)], row.at[:, pl.ds(width, width)]
        return [
            pltpu.make_async_copy(clean, sides[f].at[k], sem_out.at[step]),
            pltpu.make_async_copy(corrupt, outs[k].at[f], sem_out.at[rows + step]),
        ]

    def emit(step, carry):
        make_row(step)
        for k in range(X):
            for f in range(ZL):

                @pl.when(step == k * ZL + f)
                def _(k=k, f=f):
                    for copy in leave(k, f):
                        copy.start()

        return carry

    lax.fori_loop(0, rows, emit, 0)
    own_copy.wait()
    for k in range(X):
        for f in range(ZL):
            for copy in leave(k, f):
                copy.wait()


def products(split, meta, normed, other_normed, pieces):
    slots, block_len, _ = normed.shape
    width = pieces[0].shape[2]
    outs = [jax.ShapeDtypeStruct((ZL, block_len, width if split else 2 * width), jnp.bfloat16)] * X
    if split:
        outs = [jax.ShapeDtypeStruct((X, block_len, width), jnp.bfloat16)] * ZL + outs
    return pl.pallas_call(
        functools.partial(products_kernel, split),
        in_specs=[pl.BlockSpec(memory_space=pltpu.SMEM)]
        + [pl.BlockSpec(memory_space=pl.ANY)] * (2 + len(pieces)),
        out_specs=[pl.BlockSpec(memory_space=pl.ANY)] * (len(outs) + 1),
        out_shape=outs + [jax.ShapeDtypeStruct((block_len, width), jnp.bfloat16)],
        scratch_shapes=[
            pltpu.VMEM((CORES * Y * ZH, block_len, width), jnp.bfloat16),
            pltpu.VMEM((CORES * slots, block_len, block_len), normed.dtype),
            pltpu.VMEM((X * ZL, block_len, 2 * width), jnp.bfloat16),
            pltpu.VMEM((block_len, 2 * width), jnp.float32),
            pltpu.SemaphoreType.DMA((CORES * Y * ZH,)),
            pltpu.SemaphoreType.DMA((CORES * slots,)),
            pltpu.SemaphoreType.DMA((2 * X * ZL + 1,)),
        ],
        compiler_params=pltpu.CompilerParams(vmem_limit_bytes=60 * MIB),
        cost_estimate=pl.CostEstimate(
            flops=slots * block_len * block_len * 4 * width,
            bytes_accessed=10 * MIB,
            transcendentals=0,
        ),
    )(meta, normed, other_normed, *pieces)


def finish_kernel(degree, bias, *refs):
    joint, apart, (clean, corrupt, hidden, spread) = refs[: X + 3], refs[X + 3 : -4], refs[-4:]
    scale = degree[...]
    offset = bias[...]

    def total(values):
        result = values[0].astype(jnp.float32)
        for value in values[1:]:
            result += value.astype(jnp.float32)
        return result

    def write(out, sums, own, columns):
        value = sums + own[...].astype(jnp.float32) / scale + offset[:, columns]
        out[:, columns] = jnp.maximum(value, 0.0)

    *parts, last, own, own_corrupt = joint
    width = own.shape[1]
    sums = total([ref[0] for ref in parts] + [last[...]])
    write(clean, sums[:, :width], own, slice(0, width))
    write(corrupt, sums[:, width:], own_corrupt, slice(0, width))
    parts, (last, own, own_corrupt) = apart[: 2 * X], apart[2 * X :]
    write(clean, total([ref[...] for ref in parts[:X]]), own, slice(width, 2 * width))
    sums = total([ref[0] for ref in parts[X:]] + [last[...]])
    write(corrupt, sums, own_corrupt, slice(width, 2 * width))
    final = clean[...]
    hidden[...] = final.astype(hidden.dtype)
    sums = jnp.sum(final, axis=0, keepdims=True).astype(spread.dtype)
    for at in range(spread.shape[1]):
        part = sums[:, at * LANES : (at + 1) * LANES][None]
        spread[:, at : at + 1, :] = jnp.broadcast_to(part, (spread.shape[0], 1, LANES))


def finish(devices, degree, bias, joint, apart):
    block_len, hidden = degree.shape[0], bias.shape[1]
    width = hidden // 2

    def whole(*shape):
        return pl.BlockSpec(shape, lambda i: (0,) * len(shape))

    half = [whole(block_len, width)]
    return pl.pallas_call(
        finish_kernel,
        grid=(1,),
        in_specs=[whole(block_len, 1), whole(1, hidden)]
        + [whole(1, block_len, hidden)] * X
        + [whole(block_len, hidden)]
        + half * (2 + X)
        + [whole(1, block_len, width)] * X
        + half * 3,
        out_specs=[whole(block_len, hidden)] * 3 + [whole(devices, hidden // LANES, LANES)],
        out_shape=[
            jax.ShapeDtypeStruct((block_len, hidden), jnp.float32),
            jax.ShapeDtypeStruct((block_len, hidden), jnp.float32),
            jax.ShapeDtypeStruct((block_len, hidden), jnp.bfloat16),
            jax.ShapeDtypeStruct((devices, hidden // LANES, LANES), jnp.bfloat16),
        ],
        compiler_params=pltpu.CompilerParams(vmem_limit_bytes=60 * MIB),
    )(degree, bias, *joint, *apart)


def score_kernel(nodes, gathered, disc_weight, clean, corrupt, scores, spread):
    column_total = jnp.sum(gathered[...].astype(jnp.float32), axis=0)
    pieces = [column_total[at : at + 1] for at in range(column_total.shape[0])]
    summary = jax.nn.sigmoid(jnp.concatenate(pieces, axis=1) / nodes)
    lanes = (((1,), (1,)), ((), ()))
    exact = dict(precision=lax.Precision.HIGHEST, preferred_element_type=jnp.float32)
    summary = jnp.broadcast_to(summary, (8, summary.shape[1]))
    probe = lax.dot_general(summary, disc_weight[...], lanes, **exact)
    clean_score = lax.dot_general(probe, clean[...], lanes, **exact)[:1]
    corrupt_score = lax.dot_general(probe, corrupt[...], lanes, **exact)[:1]
    scores[0:1] = clean_score
    scores[1:2] = corrupt_score

    def softplus(value):
        return jnp.maximum(value, 0.0) + jnp.log1p(jnp.exp(-jnp.abs(value)))

    terms = softplus(-clean_score) + softplus(corrupt_score)
    spread[...] = jnp.broadcast_to(jnp.sum(terms, axis=1, keepdims=True), spread.shape)


def score(nodes, devices, gathered, disc_weight, clean, corrupt):
    block_len = clean.shape[0]
    return pl.pallas_call(
        functools.partial(score_kernel, nodes),
        out_shape=[
            jax.ShapeDtypeStruct((2, block_len), jnp.float32),
            jax.ShapeDtypeStruct((devices, 128), jnp.float32),
        ],
        compiler_params=pltpu.CompilerParams(vmem_limit_bytes=60 * MIB),
    )(gathered, disc_weight, clean, corrupt)


def infomax(
    features,
    proj_weight,
    bias,
    disc_weight,
    adjacency,
    row_block,
    col_block,
    block_count,
    degree,
    corrupt_source,
):
    block_len = adjacency.shape[-1]
    hidden = proj_weight.shape[1]
    wide_size = lax.axis_size("wide")
    narrow_size = lax.axis_size("narrow")
    devices = wide_size * narrow_size
    wide_at = lax.axis_index("wide")
    narrow_at = lax.axis_index("narrow")
    y, zh = wide_at // ZH, wide_at % ZH
    x, zl, core = narrow_at // (ZL * CORES), narrow_at // CORES % ZL, narrow_at % CORES
    chunks = 2
    width = hidden // chunks

    own = []
    panels = []
    for h in range(chunks):
        weight = proj_weight[:, h * width : (h + 1) * width]
        part = jnp.dot(features, weight, preferred_element_type=jnp.float32)
        part = part.astype(jnp.bfloat16)
        own.append(part)
        along_z = [part]
        for k in range(1, ZH):
            along_z.append(to_wide(part, dz=k))
        along_z = jnp.stack(along_z)
        panel = [along_z]
        for k in range(1, Y):
            panel.append(to_wide(along_z, dy=k))
        panels.append(panel)

    inv_root = lax.rsqrt(degree.astype(jnp.float32))
    col_roots = lax.dynamic_index_in_dim(
        inv_root.reshape(wide_size, narrow_size, block_len), narrow_at, 1, keepdims=False
    )
    row_roots = lax.dynamic_index_in_dim(
        inv_root.reshape(wide_size, narrow_size, block_len), wide_at, 0, keepdims=False
    )
    slot_rows = row_block[0, 0]
    slot_cols = col_block[0, 0]
    slot_row_roots = row_roots[slot_rows]
    slot_col_roots = col_roots[slot_cols]
    normed = (
        adjacency[0, 0].astype(jnp.float32)
        * slot_row_roots[:, :, None]
        * slot_col_roots[:, None, :]
    ).astype(jnp.bfloat16)

    other_normed = to_narrow(normed, flip_core=1)

    slot_ids = jnp.arange(SLOTS, dtype=jnp.int32)
    columns = jnp.arange(wide_size, dtype=jnp.int32)
    sources = (
        lax.dynamic_index_in_dim(
            corrupt_source.reshape(wide_size, narrow_size), narrow_at, 1, keepdims=False
        )
        // narrow_size
    )
    tile = jnp.concatenate(
        [
            jnp.where(slot_ids < block_count[0, 0], slot_rows, narrow_size),
            slot_cols,
            jnp.sum(jnp.where(slot_cols[:, None] == columns[None, :], sources[None, :], 0), axis=1),
        ]
    )
    other = to_narrow(tile, flip_core=1)
    keys = jnp.concatenate([tile[:SLOTS], other[:SLOTS]])
    both_cols = jnp.concatenate([tile[SLOTS : 2 * SLOTS], other[SLOTS : 2 * SLOTS] + wide_size])
    both_sources = jnp.concatenate([tile[2 * SLOTS :], other[2 * SLOTS :] + wide_size])
    ids = jnp.arange(CORES * SLOTS, dtype=jnp.int32)
    before = (keys[None, :] < keys[:, None]) | (
        (keys[None, :] == keys[:, None]) & (ids[None, :] < ids[:, None])
    )
    rank = jnp.sum(before.astype(jnp.int32), axis=1)
    order = jnp.sum(jnp.where(rank[None, :] == ids[:, None], ids[None, :], 0), axis=1)
    starts = jnp.sum(
        (keys[None, :] < jnp.arange(narrow_size + 1, dtype=jnp.int32)[:, None]).astype(jnp.int32),
        axis=1,
    )
    own_source = jnp.sum(jnp.where(columns == wide_at, sources, 0))
    steps_x = jnp.arange(X, dtype=jnp.int32)
    flips = jnp.arange(ZL, dtype=jnp.int32)
    targets = ((x + steps_x)[:, None] % X * ZL + (zl ^ flips)[None, :]) * CORES + core
    dest = (y - jnp.arange(Y, dtype=jnp.int32))[:, None] % Y * ZH + (
        zh - jnp.arange(ZH, dtype=jnp.int32)
    )[None, :] % ZH
    parts = [
        order,
        both_cols,
        both_sources,
        starts,
        targets.reshape(-1),
        dest.reshape(-1),
        own_source[None],
    ]
    parts.append(jnp.zeros((META - sum(part.shape[0] for part in parts),), jnp.int32))
    meta = jnp.concatenate([part.astype(jnp.int32) for part in parts])

    groups = []
    for h in range(chunks):
        other_panel = []
        for k in range(Y):
            other_panel.append(to_narrow(panels[h][k], flip_core=1))
        split = h == chunks - 1
        *halves, own_corrupt = products(split, meta, normed, other_normed, panels[h] + other_panel)
        clean = []
        if split:
            near, far, *halves = halves
            far = to_narrow(far, flip_z=1)
        got = [halves[0]]
        for k in range(1, X):
            got.append(to_narrow(halves[k], dx=k))
        if split:
            for k in range(X):
                part = near[k].astype(jnp.float32) + far[k].astype(jnp.float32)
                part = part.astype(jnp.bfloat16)
                clean.append(to_narrow(part, dx=k) if k else part)
        far = sum(value[1].astype(jnp.float32) for value in got).astype(jnp.bfloat16)
        last = to_narrow(far, flip_z=1)
        groups.append(clean + got + [last, own[h], own_corrupt])

    own_degree = lax.dynamic_index_in_dim(
        degree.reshape(devices, block_len), wide_at * narrow_size + narrow_at, 0, keepdims=False
    )
    degree_float = own_degree.astype(jnp.float32)[:, None]
    nodes = block_len * devices
    clean_h, corrupt_h, hidden_out, spread = finish(devices, degree_float, bias[None, :], *groups)
    gathered = lax.all_to_all(spread, BOTH, 0, 0)
    scores, spread = score(nodes, devices, gathered, disc_weight, clean_h, corrupt_h)
    gathered = lax.all_to_all(spread, BOTH, 0, 0, tiled=True)
    loss = jnp.sum(gathered[:, 0]) / (2 * nodes)
    return (hidden_out, scores, loss)


def solution(mesh):
    placed = (
        P(("wide", "narrow"), None),
        P(),
        P(),
        P(),
        P("wide", "narrow", None, None, None),
        P("wide", "narrow", None),
        P("wide", "narrow", None),
        P("wide", "narrow"),
        P(),
        P(),
    )
    return jax.shard_map(
        infomax,
        mesh=mesh,
        in_specs=placed,
        out_specs=(P(("wide", "narrow"), None), P(None, ("wide", "narrow")), P()),
        check_vma=False,
    )
```

time: 213 us -> 222 us (1.042)
  starting transfers between devices: 33.1 us -> 70 us
  waiting for transfers between devices: 64.3 us -> 48.4 us
  Pallas kernels: 35.2 us -> 24.1 us
  other arithmetic: 14.5 us -> 18.5 us
  blocking collectives: 49.8 us -> 47.4 us
    ppermute x10 -> x22, starting transfers between devices: 6.8 us -> 44.9 us  [to_narrow(): return lax.ppermute(value, 'narrow', narrow_perm(**steps))]
    pallas_call x5 -> x3, Pallas kernels: 30.8 us -> 19.6 us  [the longest x2 16 us: products(): pl.pallas_call(functools.partial(products_kernel, split), in_specs=[pl.Bl...]
    ppermute x10 -> x22, waiting for transfers between devices: 37.9 us -> 27.7 us  [to_narrow(): return lax.ppermute(value, 'narrow', narrow_perm(**steps))]
    ppermute x12, waiting for transfers between devices: 26.4 us -> 20.6 us  [to_wide(): return lax.ppermute(value, 'wide', wide_perm(**steps))]
    another operation x2, other arithmetic: 0.14 us -> 3.91 us  [infomax(): along_z = jnp.stack(along_z)]
    unnamed x37, local copies, waits for them, and re-layouts: 3.32 us -> 0.73 us
    all_to_all x1, blocking collectives: 30.7 us -> 28.3 us  [infomax(): gathered = lax.all_to_all(spread, BOTH, 0, 0)]
    convert_element_type x1 -> x2, other arithmetic: 4.49 us -> 4.37 us  [the longest x1 3.46 us: infomax(): normed = (adjacency[0, 0].astype(jnp.float32) * slot_row_roots[:, :, None...]
  transfers between devices with their start and end apart: 22 -> 34, of which waited for: 14 -> 7; matrix products, arithmetic and copies ran while one was open for 10% -> 8% of each run, Pallas kernels for 13% -> 7%
where the time goes in v2:
time: 222 us; the launch traced here: 221 us
  starting transfers between devices  70 us (32%)
  waiting for transfers between devices  48.4 us (22%)
  blocking collectives  47.4 us (21%)
  Pallas kernels  24.1 us (11%)
  other arithmetic  18.5 us (8%)
  local copies, waits for them, and re-layouts  7.48 us (3%)
  between operations  3.41 us (2%)
    ppermute x22, starting transfers between devices, to_narrow(): return lax.ppermute(value, 'narrow', narrow_perm(**steps))  44.9 us
    all_to_all x1, blocking collectives, infomax(): gathered = lax.all_to_all(spread, BOTH, 0, 0)  28.3 us
    ppermute x22, waiting for transfers between devices, to_narrow(): return lax.ppermute(value, 'narrow', narrow_perm(**steps))  27.7 us
    ppermute x12, starting transfers between devices, to_wide(): return lax.ppermute(value, 'wide', wide_perm(**steps))  25.1 us
    ppermute x12, waiting for transfers between devices, to_wide(): return lax.ppermute(value, 'wide', wide_perm(**steps))  20.6 us
    all_to_all x1, blocking collectives, infomax(): gathered = lax.all_to_all(spread, BOTH, 0, 0, tiled=True)  19.2 us
    pallas_call x2, Pallas kernels, products(): pl.pallas_call(functools.partial(products_kernel, split), in_specs=[pl.Bl...  16 us
  transfers between devices with their start and end apart: 34, of which 7 were waited for; matrix products, arithmetic and copies ran while one was open for 8% of the time, Pallas kernels for 7%

profile of v2, /device:TPU:1, one launch (start us, length us, event | category | flops | bytes accessed | tf_op | source)
XLA Modules:
  0.0 221.2 jit_solution(13240130482023894752)
XLA Ops:
  4.9 3.5 %fusion.1.normed = bf16[24,256,256]{2,1,0:T(8,128)(2,1)S(1)} fusion(s32[1,1,24,256,256]{4,3,2,1,0:T(8,128)} %param.14, f32[24,256]{1,0:T(8,128)} %gather_fusion.1, f32[24,256]{1,0:T(8,128)} %gather_fusion), kind=kLoop, calls=%fused_computation.4 | loop fusion | flops 6291456 | bytes 9486336 | tf_op jit(solution)/shard_map/convert_element_type | solution.py:341
  8.4 3.3 %collective-permute-start.1 = (bf16[24,256,256]{2,1,0:T(8,128)(2,1)S(1)}, bf16[24,256,256]{2,1,0:T(8,128)(2,1)}, u32[]{:S(2)}, u32[]{:S(2)}) collective-permute-start(bf16[24,256,256]{2,1,0:T(8,128)(2,1)S(1)} %fusion.1.normed), channel_id=1, source_target_pairs={{0,1},{1,0},{2,3},{3,2},{4,5},{5,4},{6,7},{7,6},{8,9},{9,8},{10,11... | collective-permute-start | bytes 9437192 | tf_op jit(solution)/shard_map/ppermute | solution.py:33
  13.9 5.1 %collective-permute-start.17 = (bf16[256,256]{1,0:T(8,128)(2,1)}, bf16[256,256]{1,0:T(8,128)(2,1)}, u32[]{:S(2)}, u32[]{:S(2)}) collective-permute-start(bf16[256,256]{1,0:T(8,128)(2,1)} %convolution_convert_fusion.refs_16_), channel_id=1, source_target_pairs={{0,32},{16,48},{32,0},{48,16},{64,96},{80,112},{96,64},{112,80},{1... | collective-permute-start | bytes 393224 | tf_op jit(solution)/shard_map/ppermute | solution.py:37
  23.9 6.3 %collective-permute-start.3 = (bf16[256,256]{1,0:T(8,128)(2,1)}, bf16[256,256]{1,0:T(8,128)(2,1)}, u32[]{:S(2)}, u32[]{:S(2)}) collective-permute-start(bf16[256,256]{1,0:T(8,128)(2,1)} %convolution_convert_fusion.1.refs_5_), channel_id=1, source_target_pairs={{0,32},{16,48},{32,0},{48,16},{64,96},{80,112},{96,64},{112,80},{1... | collective-permute-start | bytes 393224 | tf_op jit(solution)/shard_map/ppermute | solution.py:37
  30.2 5.3 %collective-permute-done.18 = bf16[256,256]{1,0:T(8,128)(2,1)} collective-permute-done((bf16[256,256]{1,0:T(8,128)(2,1)}, bf16[256,256]{1,0:T(8,128)(2,1)}, u32[]{:S(2)}, u32[]{:S(2)}) %collective-permute-start.18) | collective-permute-done | bytes 131104 | tf_op jit(solution)/shard_map/ppermute | solution.py:37
  38.8 2.6 %collective-permute-start.20 = (bf16[4,256,256]{2,1,0:T(8,128)(2,1)}, bf16[4,256,256]{2,1,0:T(8,128)(2,1)}, u32[]{:S(2)}, u32[]{:S(2)}) collective-permute-start(bf16[4,256,256]{2,1,0:T(8,128)(2,1)} %pad_maximum_fusion.1.refs_0_), channel_id=1, source_target_pairs={{0,128},{16,144},{32,160},{48,176},{64,192},{80,208},{96,224},{112... | collective-permute-start | bytes 1572872 | tf_op jit(solution)/shard_map/ppermute | solution.py:37
  42.1 3.3 %collective-permute-start.4 = (bf16[256,256]{1,0:T(8,128)(2,1)}, bf16[256,256]{1,0:T(8,128)(2,1)}, u32[]{:S(2)}, u32[]{:S(2)}) collective-permute-start(bf16[256,256]{1,0:T(8,128)(2,1)} %convolution_convert_fusion.1.refs_5_), channel_id=1, source_target_pairs={{0,48},{16,0},{32,16},{48,32},{64,112},{80,64},{96,80},{112,96},{1... | collective-permute-start | bytes 393224 | tf_op jit(solution)/shard_map/ppermute | solution.py:37
  47.7 3.0 %collective-permute-done.4 = bf16[256,256]{1,0:T(8,128)(2,1)} collective-permute-done((bf16[256,256]{1,0:T(8,128)(2,1)}, bf16[256,256]{1,0:T(8,128)(2,1)}, u32[]{:S(2)}, u32[]{:S(2)}) %collective-permute-start.4) | collective-permute-done | bytes 131104 | tf_op jit(solution)/shard_map/ppermute | solution.py:37
  52.7 2.8 %collective-permute-start.22 = (bf16[4,256,256]{2,1,0:T(8,128)(2,1)}, bf16[4,256,256]{2,1,0:T(8,128)(2,1)}, u32[]{:S(2)}, u32[]{:S(2)}) collective-permute-start(bf16[4,256,256]{2,1,0:T(8,128)(2,1)} %pad_maximum_fusion.1.refs_0_), channel_id=1, source_target_pairs={{0,1},{1,0},{2,3},{3,2},{4,5},{5,4},{6,7},{7,6},{8,9},{9,8},{10,11... | collective-permute-start | bytes 1572872 | tf_op jit(solution)/shard_map/ppermute | solution.py:33
  55.7 8.8 %collective-permute-done.20.refs_2_ = bf16[4,256,256]{2,1,0:T(8,128)(2,1)} collective-permute-done((bf16[4,256,256]{2,1,0:T(8,128)(2,1)}, bf16[4,256,256]{2,1,0:T(8,128)(2,1)}, u32[]{:S(2)}, u32[]{:S(2)}) %collective-permute-start.20) | collective-permute-done | bytes 524320 | tf_op jit(solution)/shard_map/ppermute | solution.py:37
  67.8 10.5 %collective-permute-start.23 = (bf16[4,256,256]{2,1,0:T(8,128)(2,1)}, bf16[4,256,256]{2,1,0:T(8,128)(2,1)}, u32[]{:S(2)}, u32[]{:S(2)}) collective-permute-start(bf16[4,256,256]{2,1,0:T(8,128)(2,1)} %collective-permute-done.19.refs_1_), channel_id=1, source_target_pairs={{0,1},{1,0},{2,3},{3,2},{4,5},{5,4},{6,7},{7,6},{8,9},{9,8},{10,11... | collective-permute-start | bytes 1572872 | tf_op jit(solution)/shard_map/ppermute | solution.py:33
  78.2 4.6 %collective-permute-start.24 = (bf16[4,256,256]{2,1,0:T(8,128)(2,1)}, bf16[4,256,256]{2,1,0:T(8,128)(2,1)}, u32[]{:S(2)}, u32[]{:S(2)}) collective-permute-start(bf16[4,256,256]{2,1,0:T(8,128)(2,1)} %collective-permute-done.20.refs_2_), channel_id=1, source_target_pairs={{0,1},{1,0},{2,3},{3,2},{4,5},{5,4},{6,7},{7,6},{8,9},{9,8},{10,11... | collective-permute-start | bytes 1572872 | tf_op jit(solution)/shard_map/ppermute | solution.py:33
  82.8 3.5 %collective-permute-done.7.refs_3_ = bf16[4,256,256]{2,1,0:T(8,128)(2,1)} collective-permute-done((bf16[4,256,256]{2,1,0:T(8,128)(2,1)}, bf16[4,256,256]{2,1,0:T(8,128)(2,1)}, u32[]{:S(2)}, u32[]{:S(2)}) %collective-permute-start.7) | collective-permute-done | bytes 524320 | tf_op jit(solution)/shard_map/ppermute | solution.py:37
  95.0 8.0 %shard_map.122 = (bf16[4,256,256]{2,1,0:T(8,128)(2,1)}, bf16[4,256,256]{2,1,0:T(8,128)(2,1)}, bf16[2,256,256]{2,1,0:T(8,128)(2,1)}, bf16[2,256,256]{2,1,0:T(8,12...) custom-call(s32[256]{0:T(256)} %concatenate.11.meta, ...), custom_call_target="tpu_custom_call" | custom-call | flops 1610612736 | bytes 10485760 | tf_op jit(solution)/shard_map/pallas_call | solution.py:170
  105.0 8.0 %shard_map.121 = (bf16[2,256,512]{2,1,0:T(8,128)(2,1)}, bf16[2,256,512]{2,1,0:T(8,128)(2,1)}, bf16[2,256,512]{2,1,0:T(8,128)(2,1)}, bf16[2,256,512]{2,1,0:T(8,128)(2,1)}, bf16[256,256]{1,0:T(8,128)(2,1)}) custom-call(s32[256]{0:T(256)} %concatenate.11.meta, bf16[24,256,256]{2,1,0:T(8,128)(2,1)} %copy-done.1, ...), custom_call_target="tpu_custom_call" | custom-call | flops 1610612736 | bytes 10485760 | tf_op jit(solution)/shard_map/pallas_call | solution.py:170
  116.7 4.5 %collective-permute-start.26 = (bf16[4,256,256]{2,1,0:T(8,128)(2,1)}, bf16[4,256,256]{2,1,0:T(8,128)(2,1)S(1)}, u32[]{:S(2)}, u32[]{:S(2)}) collective-permute-start(bf16[4,256,256]{2,1,0:T(8,128)(2,1)} %get-tuple-element.27), channel_id=1, source_target_pairs={{0,2},{1,3},{2,0},{3,1},{4,6},{5,7},{6,4},{7,5},{8,10},{9,11},{10,... | collective-permute-start | bytes 1572872 | tf_op jit(solution)/shard_map/ppermute | solution.py:33
  121.2 23.2 %collective-permute-done.32.refs_14_ = bf16[2,256,256]{2,1,0:T(8,128)(2,1)S(1)} collective-permute-done((bf16[2,256,256]{2,1,0:T(8,128)(2,1)S(1)}, bf16[2,256,256]{2,1,0:T(8,128)(2,1)S(1)}, u32[]{:S(2)}, u32[]{:S(2)}) %collective-permute-start.32) | collective-permute-done | bytes 262176 | tf_op jit(solution)/shard_map/ppermute | solution.py:33
  145.2 4.4 %collective-permute-start.33 = (bf16[256,256]{1,0:T(8,128)(2,1)}, bf16[256,256]{1,0:T(8,128)(2,1)}, u32[]{:S(2)}, u32[]{:S(2)}) collective-permute-start(bf16[256,256]{1,0:T(8,128)(2,1)} %fusion.9), channel_id=1, source_target_pairs={{0,2},{1,3},{2,0},{3,1},{4,6},{5,7},{6,4},{7,5},{8,10},{9,11},{10,... | collective-permute-start | bytes 393224 | tf_op jit(solution)/shard_map/ppermute | solution.py:33
  154.2 3.0 %collective-permute-start.28 = (bf16[256,256]{1,0:T(8,128)(2,1)}, bf16[256,256]{1,0:T(8,128)(2,1)}, u32[]{:S(2)}, u32[]{:S(2)}) collective-permute-start(bf16[256,256]{1,0:T(8,128)(2,1)} %get-tuple-element.42), channel_id=1, source_target_pairs={{0,8},{1,9},{2,10},{3,11},{4,12},{5,13},{6,14},{7,15},{8,0},{9,1},... | collective-permute-start | bytes 393224 | tf_op jit(solution)/shard_map/ppermute | solution.py:33
  158.7 3.9 %collective-permute-done.28.refs_9_ = bf16[256,256]{1,0:T(8,128)(2,1)} collective-permute-done((bf16[256,256]{1,0:T(8,128)(2,1)}, bf16[256,256]{1,0:T(8,128)(2,1)}, u32[]{:S(2)}, u32[]{:S(2)}) %collective-permute-start.28) | collective-permute-done | bytes 131104 | tf_op jit(solution)/shard_map/ppermute | solution.py:33
  163.3 3.6 %shard_map.123 = (f32[256,512]{1,0:T(8,128)}, f32[256,512]{1,0:T(8,128)}, bf16[256,512]{1,0:T(8,128)(2,1)}, bf16[256,4,128]{2,1,0:T(4,128)(2,1)}) custom-call(f32[256,1]{1,0:T(8,128)} %copy.17.degree, f32[1,512]{1,0:T(1,128)} %bitcast.60, bf16[2,256,512]{2,1,0:T(8,128)(2,1)} %get-tuple-element.21.refs_0_, bf16[2,256,512]{2,1,0:T(8,128)(2,1)} %copy-done.2, ...), custom_call_target="tpu_custom_call" | custom-call | tf_op jit(solution)/shard_map/pallas_call | solution.py:234
  166.9 28.3 %all_to_all.17.gathered = bf16[256,4,128]{2,1,0:T(4,128)(2,1)} all-to-all(bf16[256,4,128]{2,1,0:T(4,128)(2,1)} %get-tuple-element.34), channel_id=1, replica_groups=mesh['wide'=16,'narrow'=16] {'wide','narrow'}, dimensions={0} | all-to-all | bytes 524288 | tf_op jit(solution)/shard_map/all_to_all | solution.py:422
  195.2 4.4 %shard_map.124 = (f32[2,256]{1,0:T(2,128)}, f32[256,128]{1,0:T(8,128)}) custom-call(bf16[256,4,128]{2,1,0:T(4,128)(2,1)} %all_to_all.17.gathered, f32[512,512]{1,0:T(8,128)} %disc_weight.1, f32[256,512]{1,0:T(8,128)} %get-tuple-element.35.clean, f32[256,512]{1,0:T(8,128)} %get-tuple-element.36.corrupt), custom_call_target="tpu_custom_call" | custom-call | tf_op jit(solution)/shard_map/pallas_call | solution.py:276
  199.6 19.2 %all_to_all.18 = f32[256,1,128]{2,1,0:T(1,128)S(1)} all-to-all(f32[256,1,128]{2,1,0:T(1,128)} %bitcast.56), channel_id=1, replica_groups=mesh['wide'=16,'narrow'=16] {'wide','narrow'}, dimensions={0} | all-to-all | bytes 262144 | tf_op jit(solution)/shard_map/all_to_all | solution.py:424
  (128 shorter events, 44.6 us)
Async XLA Ops:
  8.4 86.6 %collective-permute-start.1 = (bf16[24,256,256]{2,1,0:T(8,128)(2,1)S(1)}, bf16[24,256,256]{2,1,0:T(8,128)(2,1)}, u32[]{:S(2)}, u32[]{:S(2)}) collective-permute-start(bf16[24,256,256]{2,1,0:T(8,128)(2,1)S(1)} %fusion.1.normed), channel_id=1, source_target_pairs={{0,1},{1,0},{2,3},{3,2},{4,5},{5,4},{6,7},{7,6},{8,9},{9,8},{10,11... | collective-permute-start | bytes 9437192 | tf_op jit(solution)/shard_map/ppermute | solution.py:33
  13.9 16.3 %collective-permute-start.17 = (bf16[256,256]{1,0:T(8,128)(2,1)}, bf16[256,256]{1,0:T(8,128)(2,1)}, u32[]{:S(2)}, u32[]{:S(2)}) collective-permute-start(bf16[256,256]{1,0:T(8,128)(2,1)} %convolution_convert_fusion.refs_16_), channel_id=1, source_target_pairs={{0,32},{16,48},{32,0},{48,16},{64,96},{80,112},{96,64},{112,80},{1... | collective-permute-start | bytes 393224 | tf_op jit(solution)/shard_map/ppermute | solution.py:37
  19.0 16.5 %collective-permute-start.18 = (bf16[256,256]{1,0:T(8,128)(2,1)}, bf16[256,256]{1,0:T(8,128)(2,1)}, u32[]{:S(2)}, u32[]{:S(2)}) collective-permute-start(bf16[256,256]{1,0:T(8,128)(2,1)} %convolution_convert_fusion.refs_16_), channel_id=1, source_target_pairs={{0,48},{16,0},{32,16},{48,32},{64,112},{80,64},{96,80},{112,96},{1... | collective-permute-start | bytes 393224 | tf_op jit(solution)/shard_map/ppermute | solution.py:37
  22.3 19.8 %collective-permute-start.2 = (bf16[256,256]{1,0:T(8,128)(2,1)}, bf16[256,256]{1,0:T(8,128)(2,1)}, u32[]{:S(2)}, u32[]{:S(2)}) collective-permute-start(bf16[256,256]{1,0:T(8,128)(2,1)} %convolution_convert_fusion.1.refs_5_), channel_id=1, source_target_pairs={{0,16},{16,32},{32,48},{48,0},{64,80},{80,96},{96,112},{112,64},{1... | collective-permute-start | bytes 393224 | tf_op jit(solution)/shard_map/ppermute | solution.py:37
  23.9 21.8 %collective-permute-start.3 = (bf16[256,256]{1,0:T(8,128)(2,1)}, bf16[256,256]{1,0:T(8,128)(2,1)}, u32[]{:S(2)}, u32[]{:S(2)}) collective-permute-start(bf16[256,256]{1,0:T(8,128)(2,1)} %convolution_convert_fusion.1.refs_5_), channel_id=1, source_target_pairs={{0,32},{16,48},{32,0},{48,16},{64,96},{80,112},{96,64},{112,80},{1... | collective-permute-start | bytes 393224 | tf_op jit(solution)/shard_map/ppermute | solution.py:37
  37.5 18.0 %collective-permute-start.19 = (bf16[4,256,256]{2,1,0:T(8,128)(2,1)}, bf16[4,256,256]{2,1,0:T(8,128)(2,1)}, u32[]{:S(2)}, u32[]{:S(2)}) collective-permute-start(bf16[4,256,256]{2,1,0:T(8,128)(2,1)} %pad_maximum_fusion.1.refs_0_), channel_id=1, source_target_pairs={{0,64},{16,80},{32,96},{48,112},{64,128},{80,144},{96,160},{112,17... | collective-permute-start | bytes 1572872 | tf_op jit(solution)/shard_map/ppermute | solution.py:37
  38.8 25.7 %collective-permute-start.20 = (bf16[4,256,256]{2,1,0:T(8,128)(2,1)}, bf16[4,256,256]{2,1,0:T(8,128)(2,1)}, u32[]{:S(2)}, u32[]{:S(2)}) collective-permute-start(bf16[4,256,256]{2,1,0:T(8,128)(2,1)} %pad_maximum_fusion.1.refs_0_), channel_id=1, source_target_pairs={{0,128},{16,144},{32,160},{48,176},{64,192},{80,208},{96,224},{112... | collective-permute-start | bytes 1572872 | tf_op jit(solution)/shard_map/ppermute | solution.py:37
  50.7 14.5 %collective-permute-start.21 = (bf16[4,256,256]{2,1,0:T(8,128)(2,1)}, bf16[4,256,256]{2,1,0:T(8,128)(2,1)}, u32[]{:S(2)}, u32[]{:S(2)}) collective-permute-start(bf16[4,256,256]{2,1,0:T(8,128)(2,1)} %pad_maximum_fusion.1.refs_0_), channel_id=1, source_target_pairs={{0,192},{16,208},{32,224},{48,240},{64,0},{80,16},{96,32},{112,48}... | collective-permute-start | bytes 1572872 | tf_op jit(solution)/shard_map/ppermute | solution.py:37
  52.7 15.1 %collective-permute-start.22 = (bf16[4,256,256]{2,1,0:T(8,128)(2,1)}, bf16[4,256,256]{2,1,0:T(8,128)(2,1)}, u32[]{:S(2)}, u32[]{:S(2)}) collective-permute-start(bf16[4,256,256]{2,1,0:T(8,128)(2,1)} %pad_maximum_fusion.1.refs_0_), channel_id=1, source_target_pairs={{0,1},{1,0},{2,3},{3,2},{4,5},{5,4},{6,7},{7,6},{8,9},{9,8},{10,11... | collective-permute-start | bytes 1572872 | tf_op jit(solution)/shard_map/ppermute | solution.py:33
  55.5 22.8 %collective-permute-start.6 = (bf16[4,256,256]{2,1,0:T(8,128)(2,1)}, bf16[4,256,256]{2,1,0:T(8,128)(2,1)}, u32[]{:S(2)}, u32[]{:S(2)}) collective-permute-start(bf16[4,256,256]{2,1,0:T(8,128)(2,1)} %pad_maximum_fusion.refs_0_), channel_id=1, source_target_pairs={{0,128},{16,144},{32,160},{48,176},{64,192},{80,208},{96,224},{112... | collective-permute-start | bytes 1572872 | tf_op jit(solution)/shard_map/ppermute | solution.py:37
  64.5 21.8 %collective-permute-start.7 = (bf16[4,256,256]{2,1,0:T(8,128)(2,1)}, bf16[4,256,256]{2,1,0:T(8,128)(2,1)}, u32[]{:S(2)}, u32[]{:S(2)}) collective-permute-start(bf16[4,256,256]{2,1,0:T(8,128)(2,1)} %pad_maximum_fusion.refs_0_), channel_id=1, source_target_pairs={{0,192},{16,208},{32,224},{48,240},{64,0},{80,16},{96,32},{112,48}... | collective-permute-start | bytes 1572872 | tf_op jit(solution)/shard_map/ppermute | solution.py:37
  65.2 25.3 %collective-permute-start.5 = (bf16[4,256,256]{2,1,0:T(8,128)(2,1)}, bf16[4,256,256]{2,1,0:T(8,128)(2,1)}, u32[]{:S(2)}, u32[]{:S(2)}) collective-permute-start(bf16[4,256,256]{2,1,0:T(8,128)(2,1)} %pad_maximum_fusion.refs_0_), channel_id=1, source_target_pairs={{0,64},{16,80},{32,96},{48,112},{64,128},{80,144},{96,160},{112,17... | collective-permute-start | bytes 1572872 | tf_op jit(solution)/shard_map/ppermute | solution.py:37
  67.8 22.8 %collective-permute-start.23 = (bf16[4,256,256]{2,1,0:T(8,128)(2,1)}, bf16[4,256,256]{2,1,0:T(8,128)(2,1)}, u32[]{:S(2)}, u32[]{:S(2)}) collective-permute-start(bf16[4,256,256]{2,1,0:T(8,128)(2,1)} %collective-permute-done.19.refs_1_), channel_id=1, source_target_pairs={{0,1},{1,0},{2,3},{3,2},{4,5},{5,4},{6,7},{7,6},{8,9},{9,8},{10,11... | collective-permute-start | bytes 1572872 | tf_op jit(solution)/shard_map/ppermute | solution.py:33
  78.2 12.8 %collective-permute-start.24 = (bf16[4,256,256]{2,1,0:T(8,128)(2,1)}, bf16[4,256,256]{2,1,0:T(8,128)(2,1)}, u32[]{:S(2)}, u32[]{:S(2)}) collective-permute-start(bf16[4,256,256]{2,1,0:T(8,128)(2,1)} %collective-permute-done.20.refs_2_), channel_id=1, source_target_pairs={{0,1},{1,0},{2,3},{3,2},{4,5},{5,4},{6,7},{7,6},{8,9},{9,8},{10,11... | collective-permute-start | bytes 1572872 | tf_op jit(solution)/shard_map/ppermute | solution.py:33
  90.6 14.4 %collective-permute-start.10 = (bf16[4,256,256]{2,1,0:T(8,128)(2,1)}, bf16[4,256,256]{2,1,0:T(8,128)(2,1)}, u32[]{:S(2)}, u32[]{:S(2)}) collective-permute-start(bf16[4,256,256]{2,1,0:T(8,128)(2,1)} %collective-permute-done.6.refs_2_), channel_id=1, source_target_pairs={{0,1},{1,0},{2,3},{3,2},{4,5},{5,4},{6,7},{7,6},{8,9},{9,8},{10,11... | collective-permute-start | bytes 1572872 | tf_op jit(solution)/shard_map/ppermute | solution.py:33
  91.1 13.9 %collective-permute-start.11 = (bf16[4,256,256]{2,1,0:T(8,128)(2,1)}, bf16[4,256,256]{2,1,0:T(8,128)(2,1)}, u32[]{:S(2)}, u32[]{:S(2)}) collective-permute-start(bf16[4,256,256]{2,1,0:T(8,128)(2,1)} %collective-permute-done.7.refs_3_), channel_id=1, source_target_pairs={{0,1},{1,0},{2,3},{3,2},{4,5},{5,4},{6,7},{7,6},{8,9},{9,8},{10,11... | collective-permute-start | bytes 1572872 | tf_op jit(solution)/shard_map/ppermute | solution.py:33
  91.2 13.8 %collective-permute-start.9 = (bf16[4,256,256]{2,1,0:T(8,128)(2,1)}, bf16[4,256,256]{2,1,0:T(8,128)(2,1)}, u32[]{:S(2)}, u32[]{:S(2)}) collective-permute-start(bf16[4,256,256]{2,1,0:T(8,128)(2,1)} %collective-permute-done.5.refs_1_), channel_id=1, source_target_pairs={{0,1},{1,0},{2,3},{3,2},{4,5},{5,4},{6,7},{7,6},{8,9},{9,8},{10,11... | collective-permute-start | bytes 1572872 | tf_op jit(solution)/shard_map/ppermute | solution.py:33
  103.3 13.5 %collective-permute-start.31 = (bf16[2,256,256]{2,1,0:T(8,128)(2,1)}, bf16[2,256,256]{2,1,0:T(8,128)(2,1)S(1)}, u32[]{:S(2)}, u32[]{:S(2)}) collective-permute-start(bf16[2,256,256]{2,1,0:T(8,128)(2,1)} %get-tuple-element.30), channel_id=1, source_target_pairs={{0,8},{1,9},{2,10},{3,11},{4,12},{5,13},{6,14},{7,15},{8,0},{9,1},... | collective-permute-start | bytes 786440 | tf_op jit(solution)/shard_map/ppermute | solution.py:33
  113.0 36.7 %collective-permute-start.12 = (bf16[2,256,512]{2,1,0:T(8,128)(2,1)}, bf16[2,256,512]{2,1,0:T(8,128)(2,1)S(1)}, u32[]{:S(2)}, u32[]{:S(2)}) collective-permute-start(bf16[2,256,512]{2,1,0:T(8,128)(2,1)} %get-tuple-element.22), channel_id=1, source_target_pairs={{0,4},{1,5},{2,6},{3,7},{4,8},{5,9},{6,10},{7,11},{8,12},{9,13},{1... | collective-permute-start | bytes 1572872 | tf_op jit(solution)/shard_map/ppermute | solution.py:33
  113.4 36.3 %collective-permute-start.13 = (bf16[2,256,512]{2,1,0:T(8,128)(2,1)}, bf16[2,256,512]{2,1,0:T(8,128)(2,1)S(1)}, u32[]{:S(2)}, u32[]{:S(2)}) collective-permute-start(bf16[2,256,512]{2,1,0:T(8,128)(2,1)} %get-tuple-element.23), channel_id=1, source_target_pairs={{0,8},{1,9},{2,10},{3,11},{4,12},{5,13},{6,14},{7,15},{8,0},{9,1},... | collective-permute-start | bytes 1572872 | tf_op jit(solution)/shard_map/ppermute | solution.py:33
  113.4 36.3 %collective-permute-start.14 = (bf16[2,256,512]{2,1,0:T(8,128)(2,1)}, bf16[2,256,512]{2,1,0:T(8,128)(2,1)S(1)}, u32[]{:S(2)}, u32[]{:S(2)}) collective-permute-start(bf16[2,256,512]{2,1,0:T(8,128)(2,1)} %get-tuple-element.24), channel_id=1, source_target_pairs={{0,12},{1,13},{2,14},{3,15},{4,0},{5,1},{6,2},{7,3},{8,4},{9,5},{1... | collective-permute-start | bytes 1572872 | tf_op jit(solution)/shard_map/ppermute | solution.py:33
  115.9 28.6 %collective-permute-start.32 = (bf16[2,256,256]{2,1,0:T(8,128)(2,1)S(1)}, bf16[2,256,256]{2,1,0:T(8,128)(2,1)S(1)}, u32[]{:S(2)}, u32[]{:S(2)}) collective-permute-start(bf16[2,256,256]{2,1,0:T(8,128)(2,1)S(1)} %copy-done.17), channel_id=1, source_target_pairs={{0,12},{1,13},{2,14},{3,15},{4,0},{5,1},{6,2},{7,3},{8,4},{9,5},{1... | collective-permute-start | bytes 786440 | tf_op jit(solution)/shard_map/ppermute | solution.py:33
  116.7 35.0 %collective-permute-start.26 = (bf16[4,256,256]{2,1,0:T(8,128)(2,1)}, bf16[4,256,256]{2,1,0:T(8,128)(2,1)S(1)}, u32[]{:S(2)}, u32[]{:S(2)}) collective-permute-start(bf16[4,256,256]{2,1,0:T(8,128)(2,1)} %get-tuple-element.27), channel_id=1, source_target_pairs={{0,2},{1,3},{2,0},{3,1},{4,6},{5,7},{6,4},{7,5},{8,10},{9,11},{10,... | collective-permute-start | bytes 1572872 | tf_op jit(solution)/shard_map/ppermute | solution.py:33
  145.2 12.9 %collective-permute-start.33 = (bf16[256,256]{1,0:T(8,128)(2,1)}, bf16[256,256]{1,0:T(8,128)(2,1)}, u32[]{:S(2)}, u32[]{:S(2)}) collective-permute-start(bf16[256,256]{1,0:T(8,128)(2,1)} %fusion.9), channel_id=1, source_target_pairs={{0,2},{1,3},{2,0},{3,1},{4,6},{5,7},{6,4},{7,5},{8,10},{9,11},{10,... | collective-permute-start | bytes 393224 | tf_op jit(solution)/shard_map/ppermute | solution.py:33
  (28 other events, 583.7 us)
